TPU v7x, 32 devices: a whole 2x2x4 slice. The times are simulated.
32 devices in a mesh: row: 8 (over y, x, core), col: 4 (over z).
Axes of the slice: x: 2, y: 2, z: 4, core: 2. Of those that a mesh axis runs over, the one named last changes fastest.
Arguments:
- multispectral: float32 [8, 256, 512], P('col', 'row'), may hold values from -6 to 6
- panchromatic: float32 [1024, 2048], P('row', 'col'), may hold values from -6 to 6
- band_gains: float32 [8, 3], replicated, may hold values from 0.5 to 2
Outputs:
- sharpened: float32 [8, 1024, 2048], P(None, 'row', 'col')
All inputs are finite; a program needn't handle non-finite values.
Results may differ from a plain program's by a relative error of at most 0.000065.
Values sent between devices are 32-bit elements; how exact they have to be, the bound alone decides.
No kernel may reach another device: no remote copies, remote signals or barrier semaphores. Data moves between devices by JAX's collectives and lax.ppermute only.
A program may use at most 128 MiB of HBM per device.

v0:
```python
import functools

import jax
import jax.numpy as jnp
import numpy as np
from jax import lax
from jax.experimental import pallas as pl
from jax.experimental.pallas import tpu as pltpu
from jax.sharding import PartitionSpec as P

LEVELS = 3
TAPS = [
    0.2303778133088964,
    0.7148465705529155,
    0.6308807679298587,
    -0.0279837694168599,
    -0.1870348117190931,
    0.0308413818355607,
    0.0328830116668852,
    -0.010597401785069,
]
REACH = 48
COEFS = 24
RIM = 16
BAND_ROWS = 56
VMEM = pltpu.VMEM
F32, BF16 = jnp.float32, jnp.bfloat16


def keys_weight(t):
    t = abs(t)
    if t <= 1.0:
        return 1.5 * t**3 - 2.5 * t**2 + 1.0
    return -0.5 * t**3 + 2.5 * t**2 - 4.0 * t + 2.0 if t < 2.0 else 0.0


def upsample_matrix(n):
    m = np.zeros((n, n // 4))
    for y in range(n):
        centre = (y + 0.5) / 4.0 - 0.5
        for k in range(int(np.floor(centre)) - 1, int(np.floor(centre)) + 3):
            m[y, k % (n // 4)] += keys_weight(centre - k)
    return m


def low_matrix(n, tree):
    taps, offset = (TAPS, 3) if tree == 0 else (TAPS[::-1], 4)
    m = np.zeros((n // 2, n))
    for k in range(n // 2):
        for j in range(8):
            m[k, (2 * k + j - offset) % n] += taps[j]
    return m


@functools.lru_cache(None)
def smooth_matrix(n, level):
    total = 0.0
    for tree in range(2):
        chain = np.eye(n)
        for step in range(level):
            chain = low_matrix(n >> step, tree) @ chain
        total = total + 0.5 * chain.T @ chain
    return total


def split_const(m):
    m = np.asarray(m, np.float32)
    hi = m.astype(BF16)
    lo = (m - hi.astype(np.float32)).astype(BF16)
    return hi, lo


@functools.lru_cache(None)
def constants(rows, cols):
    half = cols // 2
    n = 1024
    q = [smooth_matrix(n, level) for level in (1, 2, 3)]
    o = 256
    stack = lambda lo, hi: np.concatenate([m[o : o + 128, lo:hi] for m in q])
    send, recv = [], []
    for lo, hi, base in ((o - REACH, o, 0), (o + 128, o + 128 + REACH, 0)):
        u, s, vt = np.linalg.svd(stack(lo, hi), full_matrices=False)
        assert s[COEFS - 3] < 1e-14
        send.append(vt[:COEFS])
        recv.append(vt[:COEFS].T)
    below, above = send[0], send[1]
    own, edge = [], []
    for m in q:
        body = m[o : o + rows]
        own.append(body[:, o : o + rows])
        above_part = body[:REACH, o - REACH : o] @ recv[0]
        below_part = body[-REACH:, o + rows : o + rows + REACH] @ recv[1]
        nothing = np.zeros((REACH, COEFS))
        both = np.block([[above_part, nothing], [nothing, below_part]])
        hi, lo = split_const(both)
        edge.append(np.concatenate([hi, hi, lo], 1))
    c1, c2 = [], []
    for m in q:
        body = m[o : o + half]
        c1.append(body[:, o : o + half].T)
        left, right = body[:, o - REACH : o], body[:, o + half : o + half + REACH]
        nothing = np.zeros((half, COEFS))
        pad = np.zeros((half, 128 - 2 * COEFS - REACH))
        first = np.concatenate([left @ recv[0], nothing, right, pad], 1).T
        second = np.concatenate([nothing, right @ recv[1], left, pad], 1).T
        c2.append(np.stack([first, second]))
    qu = q[2] @ upsample_matrix(n)
    p = o // 4
    cu = np.concatenate(
        [
            qu[o : o + cols, p : p + cols // 4],
            qu[o : o + cols, p - RIM : p],
            qu[o : o + cols, p + cols // 4 : p + cols // 4 + RIM],
            np.zeros((cols, 128 - 2 * RIM)),
        ],
        1,
    ).T
    ru_own = split_const(qu[o : o + rows, p : p + rows // 4])
    above_part, below_part = qu[o : o + rows, p - RIM : p], qu[o : o + rows, p + rows // 4 : p + rows // 4 + RIM]
    assert not above_part[BAND_ROWS:].any() and not below_part[: rows - BAND_ROWS].any()
    nothing = np.zeros((BAND_ROWS, RIM))
    ru_rim = split_const(
        np.block([[above_part[:BAND_ROWS], nothing], [nothing, below_part[rows - BAND_ROWS :]]])
    )
    three = lambda pair: np.concatenate([pair[0], pair[0], pair[1]], 1)
    pair = lambda m: np.concatenate(split_const(m), 1)
    parts = dict(
        below=pair(below),
        above=pair(above),
        own=pair(np.concatenate(own)),
        ru_own=three(ru_own),
        ru_rim=three(ru_rim),
    )
    for level in range(LEVELS):
        parts[f"edge{level}"] = edge[level]
        parts[f"c1{level}hi"], parts[f"c1{level}lo"] = split_const(c1[level])
        for h in range(2):
            parts[f"c2{level}{h}hi"], parts[f"c2{level}{h}lo"] = split_const(c2[level][h])
    for h in range(2):
        parts[f"cu{h}hi"], parts[f"cu{h}lo"] = split_const(cu[:, h * half : (h + 1) * half])
    table, where, at = [], {}, 0
    for name, m in parts.items():
        high = -(-m.shape[0] // 16) * 16
        table.append(np.pad(np.asarray(m, np.float32), ((0, high - m.shape[0]), (0, half - m.shape[1]))))
        where[name] = (at, m.shape)
        at += high
    table = np.concatenate(table).astype(BF16)
    count = where["own"][0]
    return table, table[:count], where


class Table:
    def __init__(self, ref, where):
        self.ref, self.where = ref, where

    def __getitem__(self, name):
        at, (high, wide) = self.where[name]
        return self.ref[at : at + high, 0:wide]

    def pair(self, name):
        x = self[name]
        wide = x.shape[1] // 2
        return x[:, :wide], x[:, wide:]

    def two(self, name):
        return self[name + "hi"], self[name + "lo"]


def swap_pairs(count):
    return [(i, i ^ 1) for i in range(count)]


def odd_pairs(count):
    return [(i, (i - 1) % count if i % 2 == 0 else (i + 1) % count) for i in range(count)]


def column_steps(count):
    if count == 4:
        return [
            ([(i, i ^ k) for i in range(4)], k != 2, lambda c, k=k: c ^ k, lambda c, k=k: c ^ k)
            for k in (1, 3, 2)
        ]
    return [
        (
            [(i, (i + k) % count) for i in range(count)],
            k in (1, count - 1),
            lambda c, k=k: lax.rem(c + k, count),
            lambda c, k=k: lax.rem(c + count - k, count),
        )
        for k in [1, count - 1] + list(range(2, count - 1))
    ]


def split(x):
    hi = x.astype(BF16)
    return hi, (x - hi.astype(F32)).astype(BF16)


def dot(a, b, dims=((1,), (0,))):
    return lax.dot_general(a, b, (dims, ((), ())), preferred_element_type=F32)


def dot3(a, b, dims=((1,), (0,))):
    return dot(a[0], b[0], dims) + dot(a[1], b[0], dims) + dot(a[0], b[1], dims)


def lanes(shape):
    return lax.broadcasted_iota(jnp.int32, shape, 1)


def pack_chunk(out, ms_ref, to, count):
    bands, low = ms_ref.shape[0], ms_ref.shape[1]
    main = bands * low
    block = lambda k: pl.ds(pl.multiple_of(lax.rem(k + count, count) * 128, 128), 128)
    packed = None
    for i in range(bands):
        out[i * low : (i + 1) * low, :] = ms_ref[i, :, block(to)]
        left, right = ms_ref[i, :, block(to - 1)], ms_ref[i, :, block(to + 1)]
        rim = jnp.where(lanes(left.shape) >= 64, left, right)
        for g in range(low // RIM):
            slot = i * (low // RIM) + g
            rolled = pltpu.roll(rim[g * RIM : (g + 1) * RIM], (2 * RIM * slot + RIM) % 128, 1)
            packed = rolled if slot == 0 else jnp.where(lanes(rolled.shape) >= 2 * RIM * slot, rolled, packed)
    out[main : main + RIM, :] = packed


def pack_kernel(count, where, ms_ref, first_ref, last_ref, table_ref, *out_refs):
    c = lax.axis_index("col")
    table = Table(table_ref, where)
    main = ms_ref.shape[0] * ms_ref.shape[1]
    below, above = table.pair("below"), table.pair("above")
    for step, out in zip(column_steps(count), out_refs):
        to = step[2](c)
        pack_chunk(out, ms_ref, to, count)
        if step[1]:
            to_right = to == lax.rem(c + 1, count)
            edge = jnp.where(to_right, pltpu.roll(last_ref[...], REACH, 1), first_ref[...])
            v = tuple(jnp.where(to_right, x.astype(F32), y.astype(F32)).astype(BF16) for x, y in zip(below, above))
            out[main + RIM : main + RIM + COEFS, :] = dot3(v, split(edge[:, :REACH]), ((1,), (1,)))


def stage_kernel(count, where, ms_ref, pan_ref, table_ref, own_ref, top_ref, bot_ref):
    table = Table(table_ref, where)
    pack_chunk(own_ref, ms_ref, lax.axis_index("col"), count)
    rows = pan_ref.shape[0]
    for out, name, at in ((bot_ref, "below", rows - REACH), (top_ref, "above", 0)):
        full = dot3(table.pair(name), split(pan_ref[at : at + REACH, :]))
        for k in range(pan_ref.shape[1] // 128):
            out[k * COEFS : (k + 1) * COEFS, :] = full[:, k * 128 : (k + 1) * 128]


def rim_kernel(count, low, where, top_ref, bot_ref, table_ref, *refs):
    table = Table(table_ref, where)
    q = refs[:count]
    a_ref, b_ref, xh_ref = refs[count:]
    c, r = lax.axis_index("col"), lax.axis_index("row")
    steps = column_steps(count)
    bands = (q[0].shape[0] - RIM) // low
    main = bands * low
    even = lax.rem(r, 2) == 0
    first = q[1][main + RIM : main + RIM + COEFS, :]
    second = q[2][main + RIM : main + RIM + COEFS, :]
    first_is_right = steps[0][3](c) == lax.rem(c + 1, count)
    left = jnp.where(first_is_right, second, first)
    right = jnp.where(first_is_right, first, second)
    filler = jnp.zeros((128 - 2 * COEFS, 128), F32)
    xh = jnp.concatenate([left, right, filler], 0).T
    xh_ref[...] = xh
    height = top_ref.shape[0]
    per = low // RIM
    total = count * bands

    def fill(out, bottom):
        out[0:height, :] = (bot_ref if bottom else top_ref)[...]
        v = table.pair("below" if bottom else "above")
        edge = xh[xh.shape[0] - REACH :] if bottom else xh[:REACH]
        out[height : height + COEFS, :] = dot3(v, split(edge))
        base = height + COEFS
        packed = None
        for n in range(total):
            ref, i = q[n // bands], n % bands
            row = (i + 1) * low - RIM if bottom else i * low
            out[base + n * RIM : base + (n + 1) * RIM, :] = ref[row : row + RIM, :]
            slot = per * (i + 1) - 1 if bottom else per * i
            rim = pltpu.roll(ref[main : main + RIM, :], (2 * RIM * (n % 4 - slot)) % 128, 1)
            packed = rim if n % 4 == 0 else jnp.where(lanes(rim.shape) >= 2 * RIM * (n % 4), rim, packed)
            if n % 4 == 3 or n == total - 1:
                spot = base + total * RIM + (n // 4) * RIM
                out[spot : spot + RIM, :] = packed

    @pl.when(even)
    def _():
        fill(a_ref, 1)
        fill(b_ref, 0)

    @pl.when(jnp.logical_not(even))
    def _():
        fill(a_ref, 0)
        fill(b_ref, 1)


def own_rims(own_right, own_left, xh):
    inner = lanes(xh.shape) < 2 * COEFS
    return (
        jnp.where(inner, xh, pltpu.roll(own_right, 2 * COEFS, 1)),
        jnp.where(inner, xh, pltpu.roll(own_left, 2 * COEFS + REACH, 1)),
    )


def columns(t, cols, table, level):
    half = cols // 2
    out = []
    for h in range(2):
        own = tuple(x[:, h * half : (h + 1) * half] for x in t)
        rim = tuple(x[:, cols + h * 128 : cols + (h + 1) * 128] for x in t)
        out.append(
            dot3(own, table.two(f"c1{level}")) + dot3(rim, table.two(f"c2{level}{h}"))
        )
    return out


def low_columns(x, table):
    return jnp.concatenate([dot3(x, table.two(f"cu{h}")) for h in range(2)], 1)


def local_kernel(count, low, where, gains_ref, *refs):
    q, refs = refs[:count], refs[count:]
    pan_ref, xh_ref, table_ref, part_ref, xe, e3, mext = refs
    table = Table(table_ref, where)
    c = lax.axis_index("col")
    steps = column_steps(count)
    bands = (q[0].shape[0] - RIM) // low
    main = bands * low
    rows, cols = pan_ref.shape
    half = cols // 2
    xe[:, 0:cols] = pan_ref[...]
    f, s = own_rims(pan_ref[:, half : half + 128], pan_ref[:, half - 128 : half], xh_ref[...])
    xe[:, cols : cols + 128] = f
    xe[:, cols + 128 : cols + 256] = s
    x = split(xe[...])
    for level in range(LEVELS):
        rs = slice(level * rows, (level + 1) * rows)
        t = split(dot3(tuple(m[rs] for m in table.pair("own")), x))
        for h, e in enumerate(columns(t, cols, table, level)):
            e3[level, :, h * half : (h + 1) * half] = e
    per = low // RIM
    for n in range(count * bands):
        ref, i = q[n // bands], n % bands
        mext[n * low : (n + 1) * low, 0:128] = ref[i * low : (i + 1) * low, :]
        for g in range(per):
            at = n * low + g * RIM
            mext[at : at + RIM, 128:256] = pltpu.roll(
                ref[main : main + RIM, :], (-2 * RIM * (i * per + g)) % 128, 1
            )
    for j in range(count):
        src = c if j == 0 else steps[j - 1][3](c)
        y = low_columns(split(mext[j * main : (j + 1) * main, :]), table)
        for i in range(bands):
            band = src * bands + i
            hi, lo = split(y[i * low : (i + 1) * low])
            g1, g2, g3 = gains_ref[band, 0], gains_ref[band, 1], gains_ref[band, 2]
            part_ref[j * bands + i] = (
                dot(table["ru_own"], jnp.concatenate([hi, lo, hi], 0))
                + g1 * pan_ref[...]
                + (g2 - g1) * e3[0]
                + (g3 - g2) * e3[1]
                - g3 * e3[2]
            )


def main_kernel(count, low, bands, where, gains_ref, *refs):
    part_ref, a_ref, b_ref, table_ref, out_ref, xe, de, mext, obuf, sems = refs
    table = Table(table_ref, where)
    c, r = lax.axis_index("col"), lax.axis_index("row")
    steps = column_steps(count)
    even = lax.rem(r, 2) == 0
    total, rows, cols = part_ref.shape
    half = cols // 2
    blocks = cols // 128
    mid = half // 128
    base = (blocks + 1) * COEFS
    for ref, below in ((a_ref, even), (b_ref, jnp.logical_not(even))):
        at = pl.ds(pl.multiple_of(jnp.where(below, COEFS, 0), 8), COEFS)
        piece = lambda k: ref[k * COEFS : (k + 1) * COEFS, :]
        for k in range(blocks):
            xe[at, k * 128 : (k + 1) * 128] = piece(k)
        f, s = own_rims(piece(mid), piece(mid - 1), piece(blocks))
        xe[at, cols : cols + 128] = f
        xe[at, cols + 128 : cols + 256] = s
        for n in range(total):
            at = pl.ds(pl.multiple_of(n * 2 * RIM + jnp.where(below, RIM, 0), 16), RIM)
            mext[at, 0:128] = ref[base + n * RIM : base + (n + 1) * RIM, :]
            spot = base + total * RIM + (n // 4) * RIM
            mext[at, 128:256] = pltpu.roll(ref[spot : spot + RIM, :], (-2 * RIM * (n % 4)) % 128, 1)
    x = split(xe[...])
    for level in range(LEVELS):
        for h, z in enumerate(columns(x, cols, table, level)):
            hi, lo = split(z)
            de[level, :, h * half : (h + 1) * half] = dot(table[f"edge{level}"], jnp.concatenate([hi, lo, hi], 0))
    copies = []
    for j in range(count):
        src = c if j == 0 else steps[j - 1][3](c)
        high = bands * 2 * RIM
        y = low_columns(split(mext[j * high : (j + 1) * high, :]), table)
        for i in range(bands):
            band = src * bands + i
            n = j * bands + i
            hi, lo = split(y[i * 2 * RIM : (i + 1) * 2 * RIM])
            g1, g2, g3 = gains_ref[band, 0], gains_ref[band, 1], gains_ref[band, 2]
            add = dot(table["ru_rim"], jnp.concatenate([hi, lo, hi], 0))
            fix = (g2 - g1) * de[0] + (g3 - g2) * de[1] - g3 * de[2]
            top = add[:BAND_ROWS]
            top = jnp.concatenate([top[:REACH] + fix[:REACH], top[REACH:]], 0)
            low_end = add[BAND_ROWS:]
            low_end = jnp.concatenate(
                [low_end[: BAND_ROWS - REACH], low_end[BAND_ROWS - REACH :] + fix[REACH:]], 0
            )
            obuf[n, 0:BAND_ROWS] = part_ref[n, 0:BAND_ROWS] + top
            obuf[n, BAND_ROWS : rows - BAND_ROWS] = part_ref[n, BAND_ROWS : rows - BAND_ROWS]
            obuf[n, rows - BAND_ROWS :] = part_ref[n, rows - BAND_ROWS :] + low_end
            copy = pltpu.make_async_copy(obuf.at[n], out_ref.at[band], sems.at[n])
            copy.start()
            copies.append(copy)
    for copy in copies:
        copy.wait()


def on_device(multispectral, panchromatic, band_gains):
    count, row_count = lax.axis_size("col"), lax.axis_size("row")
    bands, low, _ = multispectral.shape
    rows, cols = panchromatic.shape
    total = count * bands
    table, small, where = constants(rows, cols)
    steps = column_steps(count)
    chunk = bands * low + RIM
    shape = lambda n, m=128: jax.ShapeDtypeStruct((n, m), F32)
    whole = pl.BlockSpec(memory_space=VMEM)
    heights = [chunk + (COEFS if step[1] else 0) for step in steps]
    last = cols // 128 - 1
    packed = pl.pallas_call(
        functools.partial(pack_kernel, count, where),
        out_shape=[shape(h) for h in heights],
        grid=(1,),
        in_specs=[
            pl.BlockSpec(multispectral.shape, lambda i: (0, 0, 0)),
            pl.BlockSpec((rows, 128), lambda i: (0, 0)),
            pl.BlockSpec((rows, 128), lambda i: (0, last)),
            pl.BlockSpec(small.shape, lambda i: (0, 0)),
        ],
        out_specs=[pl.BlockSpec((h, 128), lambda i: (0, 0)) for h in heights],
        name="pack",
    )(multispectral, panchromatic, panchromatic, jnp.asarray(small))
    params = lambda mib: pltpu.CompilerParams(vmem_limit_bytes=mib << 20)
    cost = lambda flops: pl.CostEstimate(flops=flops, bytes_accessed=10**6, transcendentals=0)
    table = jnp.asarray(table)
    height = cols // 128 * COEFS
    own, top, bot = pl.pallas_call(
        functools.partial(stage_kernel, count, where),
        out_shape=[shape(chunk), shape(height), shape(height)],
        in_specs=[whole] * 3,
        out_specs=[whole] * 3,
        compiler_params=params(8),
        cost_estimate=cost(10**9),
        name="stage",
    )(multispectral, panchromatic, table)
    q = [own] + [lax.ppermute(x, "col", step[0]) for x, step in zip(packed, steps)]
    sent = height + COEFS + total * RIM + -(-total // 4) * RIM
    a, b, xh = pl.pallas_call(
        functools.partial(rim_kernel, count, low, where),
        out_shape=[shape(sent), shape(sent), shape(rows)],
        in_specs=[whole] * (3 + count),
        out_specs=[whole] * 3,
        compiler_params=params(8),
        name="rim",
    )(top, bot, table, *q)
    a = lax.ppermute(a, "row", swap_pairs(row_count))
    b = lax.ppermute(b, "row", odd_pairs(row_count))
    smem = pl.BlockSpec(memory_space=pltpu.SMEM)
    part = pl.pallas_call(
        functools.partial(local_kernel, count, low, where),
        out_shape=jax.ShapeDtypeStruct((total, rows, cols), F32),
        in_specs=[smem] + [whole] * (count + 3),
        out_specs=whole,
        scratch_shapes=[
            VMEM((rows, cols + 256), F32),
            VMEM((LEVELS, rows, cols), F32),
            VMEM((total * low, 256), F32),
        ],
        compiler_params=params(16),
        cost_estimate=cost(4 * 10**9),
        name="local",
    )(band_gains, *q, panchromatic, xh, table)
    return pl.pallas_call(
        functools.partial(main_kernel, count, low, bands, where),
        out_shape=jax.ShapeDtypeStruct((total, rows, cols), F32),
        in_specs=[smem] + [whole] * 4,
        out_specs=pl.BlockSpec(memory_space=pltpu.HBM),
        scratch_shapes=[
            VMEM((2 * COEFS, cols + 256), F32),
            VMEM((LEVELS, 2 * REACH, cols), F32),
            VMEM((total * 2 * RIM, 256), F32),
            VMEM((total, rows, cols), F32),
            pltpu.SemaphoreType.DMA((total,)),
        ],
        compiler_params=params(16),
        name="combine",
    )(band_gains, part, a, b, table)


def solution(mesh):
    in_specs = (P("col", "row", None), P("row", "col"), P())
    out_specs = P(None, "row", "col")
    return jax.shard_map(
        on_device, mesh=mesh, in_specs=in_specs, out_specs=out_specs, check_vma=False
    )
```

profile of v0, /device:TPU:0, one launch (start us, length us, event | category | flops | bytes accessed | tf_op | source)
XLA Modules:
  0.0 24.2 jit_solution(5010342016467685818)
XLA Ops:
  0.0 0.0 copy-start.5
  0.0 1.9 %pack.1 = (f32[104,128]{1,0:T(8,128)}, f32[104,128]{1,0:T(8,128)}, f32[80,128]{1,0:T(8,128)}) custom-call(f32[2,32,512]{2,1,0:T(8,128)} %ms_ref.3, f32[128,512]{1,0:T(8,128)} %refs_4_.1, f32[128,512]{1,0:T(8,128)} %refs_4_.1, bf16[64,256]{1,0:T(8,128)(2,1)} %constant.4.clone.table_ref), custom_call_target="tpu_custom_call" | custom-call | tf_op jit(solution)/shard_map/pack/pallas_call | solution.py:440
  1.9 4.1 %collective-permute-start.2 = (f32[80,128]{1,0:T(8,128)}, f32[80,128]{1,0:T(8,128)S(1)}, u32[]{:S(2)}, u32[]{:S(2)}) collective-permute-start(f32[80,128]{1,0:T(8,128)} %get-tuple-element.17), channel_id=1, source_target_pairs={{0,2},{1,3},{2,0},{3,1},{4,6},{5,7},{6,4},{7,5},{8,10},{9,11},{10,... | collective-permute-start | bytes 122888 | tf_op jit(solution)/shard_map/ppermute | solution.py:466
  6.0 1.6 %collective-permute-start = (f32[104,128]{1,0:T(8,128)}, f32[104,128]{1,0:T(8,128)S(1)}, u32[]{:S(2)}, u32[]{:S(2)}) collective-permute-start(f32[104,128]{1,0:T(8,128)} %get-tuple-element.15), channel_id=1, source_target_pairs={{0,1},{1,0},{2,3},{3,2},{4,5},{5,4},{6,7},{7,6},{8,9},{9,8},{10,11... | collective-permute-start | bytes 159752 | tf_op jit(solution)/shard_map/ppermute | solution.py:466
  7.5 0.0 collective-permute-start.1
  7.5 0.0 copy-start
  7.5 1.7 %copy-done = bf16[5072,256]{1,0:T(8,128)(2,1)S(1)} copy-done((bf16[5072,256]{1,0:T(8,128)(2,1)S(1)}, bf16[5072,256]{1,0:T(8,128)(2,1)}, u32[]{:S(2)}) %copy-start) | copy-done | bytes 2596888
  9.3 0.0 copy-start.2
  9.3 0.9 %copy-done.2 = f32[128,512]{1,0:T(8,128)S(1)} copy-done((f32[128,512]{1,0:T(8,128)S(1)}, f32[128,512]{1,0:T(8,128)}, u32[]{:S(2)}) %copy-start.2) | copy-done | bytes 262168
  10.2 0.0 copy-start.4
  10.2 0.9 %copy-done.4 = f32[2,32,512]{2,1,0:T(8,128)S(1)} copy-done((f32[2,32,512]{2,1,0:T(8,128)S(1)}, f32[2,32,512]{2,1,0:T(8,128)}, u32[]{:S(2)}) %copy-start.4) | copy-done | bytes 131096
  11.1 0.0 copy-start.1
  11.1 0.2 stage.1
  11.4 0.0 copy-done.5
  11.4 0.0 copy-start.3
  11.4 0.1 copy.7.gains_ref
  11.5 0.0 collective-permute-done.2.refs_3_
  11.5 0.0 collective-permute-done.refs_1_
  11.5 2.2 %collective-permute-done.1.refs_2_ = f32[104,128]{1,0:T(8,128)S(1)} collective-permute-done((f32[104,128]{1,0:T(8,128)}, f32[104,128]{1,0:T(8,128)S(1)}, u32[]{:S(2)}, u32[]{:S(2)}) %collective-permute-start.1) | collective-permute-done | bytes 53280 | tf_op jit(solution)/shard_map/ppermute | solution.py:466
  13.7 0.0 copy-done.1
  13.7 0.3 %rim.1 = (f32[280,128]{1,0:T(8,128)S(1)}, f32[280,128]{1,0:T(8,128)S(1)}, f32[128,128]{1,0:T(8,128)S(1)}) custom-call(f32[96,128]{1,0:T(8,128)S(1)} %get-tuple-element.18.top_ref, f32[96,128]{1,0:T(8,128)S(1)} %get-tuple-element.19.bot_ref, bf16[5072,256]{1,0:T(8,128)(2,1)S(1)} %copy-done.1, f32[80,128]{1,0:T(8,128)S(1)} %get-tuple-element.14.refs_0_, ...), custom_call_target="tpu_custom_call" | custom-call | tf_op jit(solution)/shard_map/rim/pallas_call | solution.py:468
  13.9 0.0 collective-permute-start.3
  14.0 2.6 %collective-permute-start.4 = (f32[280,128]{1,0:T(8,128)S(1)}, f32[280,128]{1,0:T(8,128)S(1)}, u32[]{:S(2)}, u32[]{:S(2)}) collective-permute-start(f32[280,128]{1,0:T(8,128)S(1)} %get-tuple-element.22), channel_id=1, source_target_pairs={{0,28},{4,8},{8,4},{12,16},{16,12},{20,24},{24,20},{28,0},{1,29},{... | collective-permute-start | bytes 430088 | tf_op jit(solution)/shard_map/ppermute | solution.py:477
  16.5 0.0 copy-done.3
  16.5 3.7 %local.1.refs_0_ = f32[8,128,512]{2,1,0:T(8,128)S(1)} custom-call(f32[8,3]{1,0:T(8,128)S(1)} %copy.7.gains_ref, f32[80,128]{1,0:T(8,128)S(1)} %get-tuple-element.14.refs_0_, f32[104,128]{1,0:T(8,128)S(1)} %collective-permute-done.refs_1_, f32[104,128]{1,0:T(8,128)S(1)} %collective-permute-done.1.refs_2_, f32[80,128]{1,0:T(8,128)S(1)} %collective-permute-done.2.refs_3_, ...), custom_call_target="tpu_custom_call" | custom-call | flops 4000000000 | bytes 1000000 | tf_op jit(solution)/shard_map/local/pallas_call | solution.py:479
  20.3 0.0 collective-permute-done.3.refs_1_
  20.3 0.0 collective-permute-done.4.refs_2_
  20.3 3.9 %combine.1 = f32[8,128,512]{2,1,0:T(8,128)} custom-call(f32[8,3]{1,0:T(8,128)S(1)} %copy.7.gains_ref, f32[8,128,512]{2,1,0:T(8,128)S(1)} %local.1.refs_0_, f32[280,128]{1,0:T(8,128)S(1)} %collective-permute-done.3.refs_1_, f32[280,128]{1,0:T(8,128)S(1)} %collective-permute-done.4.refs_2_, bf16[5072,256]{1,0:T(8,128)(2,1)S(1)} %copy-done.1), custom_call_target="tpu_custom_call" | custom-call | tf_op jit(solution)/shard_map/combine/pallas_call | solution.py:493
Async XLA Ops:
  0.0 11.4 %copy-start.5 = (f32[8,3]{0,1:T(4,128)S(1)}, f32[8,3]{0,1:T(4,128)}, u32[]{:S(2)}) copy-start(f32[8,3]{0,1:T(4,128)} %param.7) | copy-start | bytes 292
  1.9 9.6 %collective-permute-start.2 = (f32[80,128]{1,0:T(8,128)}, f32[80,128]{1,0:T(8,128)S(1)}, u32[]{:S(2)}, u32[]{:S(2)}) collective-permute-start(f32[80,128]{1,0:T(8,128)} %get-tuple-element.17), channel_id=1, source_target_pairs={{0,2},{1,3},{2,0},{3,1},{4,6},{5,7},{6,4},{7,5},{8,10},{9,11},{10,... | collective-permute-start | bytes 122888 | tf_op jit(solution)/shard_map/ppermute | solution.py:466
  6.0 5.5 %collective-permute-start = (f32[104,128]{1,0:T(8,128)}, f32[104,128]{1,0:T(8,128)S(1)}, u32[]{:S(2)}, u32[]{:S(2)}) collective-permute-start(f32[104,128]{1,0:T(8,128)} %get-tuple-element.15), channel_id=1, source_target_pairs={{0,1},{1,0},{2,3},{3,2},{4,5},{5,4},{6,7},{7,6},{8,9},{9,8},{10,11... | collective-permute-start | bytes 159752 | tf_op jit(solution)/shard_map/ppermute | solution.py:466
  7.5 6.1 %collective-permute-start.1 = (f32[104,128]{1,0:T(8,128)}, f32[104,128]{1,0:T(8,128)S(1)}, u32[]{:S(2)}, u32[]{:S(2)}) collective-permute-start(f32[104,128]{1,0:T(8,128)} %get-tuple-element.16), channel_id=1, source_target_pairs={{0,3},{1,2},{2,1},{3,0},{4,7},{5,6},{6,5},{7,4},{8,11},{9,10},{10,... | collective-permute-start | bytes 159752 | tf_op jit(solution)/shard_map/ppermute | solution.py:466
  7.5 1.7 %copy-start = (bf16[5072,256]{1,0:T(8,128)(2,1)S(1)}, bf16[5072,256]{1,0:T(8,128)(2,1)}, u32[]{:S(2)}) copy-start(bf16[5072,256]{1,0:T(8,128)(2,1)} %constant.5.clone.table_ref.refs_6_.refs_3_) | copy-start | bytes 7790596
  9.3 0.9 %copy-start.2 = (f32[128,512]{1,0:T(8,128)S(1)}, f32[128,512]{1,0:T(8,128)}, u32[]{:S(2)}) copy-start(f32[128,512]{1,0:T(8,128)} %refs_4_.1) | copy-start | bytes 786436
  10.2 0.9 %copy-start.4 = (f32[2,32,512]{2,1,0:T(8,128)S(1)}, f32[2,32,512]{2,1,0:T(8,128)}, u32[]{:S(2)}) copy-start(f32[2,32,512]{2,1,0:T(8,128)} %ms_ref.3) | copy-start | bytes 393220
  11.1 2.6 %copy-start.1 = (bf16[5072,256]{1,0:T(8,128)(2,1)S(1)}, bf16[5072,256]{1,0:T(8,128)(2,1)}, u32[]{:S(2)}) copy-start(bf16[5072,256]{1,0:T(8,128)(2,1)} %constant.5.clone.table_ref.refs_6_.refs_3_) | copy-start | bytes 7790596
  11.4 5.1 %copy-start.3 = (f32[128,512]{1,0:T(8,128)S(1)}, f32[128,512]{1,0:T(8,128)}, u32[]{:S(2)}) copy-start(f32[128,512]{1,0:T(8,128)} %refs_4_.1) | copy-start | bytes 786436
  13.9 6.3 %collective-permute-start.3 = (f32[280,128]{1,0:T(8,128)S(1)}, f32[280,128]{1,0:T(8,128)S(1)}, u32[]{:S(2)}, u32[]{:S(2)}) collective-permute-start(f32[280,128]{1,0:T(8,128)S(1)} %get-tuple-element.21), channel_id=1, source_target_pairs={{0,4},{4,0},{8,12},{12,8},{16,20},{20,16},{24,28},{28,24},{1,5},{5... | collective-permute-start | bytes 430088 | tf_op jit(solution)/shard_map/ppermute | solution.py:476
  14.0 6.4 %collective-permute-start.4 = (f32[280,128]{1,0:T(8,128)S(1)}, f32[280,128]{1,0:T(8,128)S(1)}, u32[]{:S(2)}, u32[]{:S(2)}) collective-permute-start(f32[280,128]{1,0:T(8,128)S(1)} %get-tuple-element.22), channel_id=1, source_target_pairs={{0,28},{4,8},{8,4},{12,16},{16,12},{20,24},{24,20},{28,0},{1,29},{... | collective-permute-start | bytes 430088 | tf_op jit(solution)/shard_map/ppermute | solution.py:477
where the time goes:
time: 24.4 us; the launch traced here: 24.2 us
  Pallas kernels  10 us (41%)
  starting transfers between devices  8.2 us (34%)
  local copies, waits for them, and re-layouts  3.68 us (15%)
  waiting for transfers between devices  2.25 us (9%)
    ppermute x3, starting transfers between devices, on_device(): lax.ppermute(x, 'col', step[0])  5.64 us
    pallas_call x1, Pallas kernels, on_device(): pl.pallas_call(functools.partial(main_kernel, count, low, bands, where),...  3.89 us
    pallas_call x1, Pallas kernels, on_device(): pl.pallas_call(functools.partial(local_kernel, count, low, where), out_sh...  3.75 us
    unnamed x13, local copies, waits for them, and re-layouts  3.68 us
    ppermute x1, starting transfers between devices, on_device(): b = lax.ppermute(b, 'row', odd_pairs(row_count))  2.55 us
    ppermute x3, waiting for transfers between devices, on_device(): lax.ppermute(x, 'col', step[0])  2.22 us
    pallas_call x1, Pallas kernels, on_device(): pl.pallas_call(functools.partial(pack_kernel, count, where), out_shape=[s...  1.89 us
  transfers between devices with their start and end apart: 5, of which 1 were waited for; matrix products, arithmetic and copies ran while one was open for 0% of the time, Pallas kernels for 16%

commit v1 on v0

--- a/solution.py
+++ b/solution.py
@@ -84,55 +84,51 @@
         send.append(vt[:COEFS])
         recv.append(vt[:COEFS].T)
     below, above = send[0], send[1]
-    own, edge = [], []
+    own, edge = [], ([], [])
     for m in q:
         body = m[o : o + rows]
         own.append(body[:, o : o + rows])
-        above_part = body[:REACH, o - REACH : o] @ recv[0]
-        below_part = body[-REACH:, o + rows : o + rows + REACH] @ recv[1]
-        nothing = np.zeros((REACH, COEFS))
-        both = np.block([[above_part, nothing], [nothing, below_part]])
-        hi, lo = split_const(both)
-        edge.append(np.concatenate([hi, hi, lo], 1))
+        edge[0].append(body[:REACH, o - REACH : o] @ recv[0])
+        edge[1].append(body[-REACH:, o + rows : o + rows + REACH] @ recv[1])
     c1, c2 = [], []
     for m in q:
         body = m[o : o + half]
         c1.append(body[:, o : o + half].T)
         left, right = body[:, o - REACH : o], body[:, o + half : o + half + REACH]
         nothing = np.zeros((half, COEFS))
-        pad = np.zeros((half, 128 - 2 * COEFS - REACH))
-        first = np.concatenate([left @ recv[0], nothing, right, pad], 1).T
-        second = np.concatenate([nothing, right @ recv[1], left, pad], 1).T
-        c2.append(np.stack([first, second]))
+        first = np.concatenate([left @ recv[0], nothing, right], 1).T
+        second = np.concatenate([nothing, right @ recv[1], left], 1).T
+        c2.append((first, second))
     qu = q[2] @ upsample_matrix(n)
     p = o // 4
+    low = rows // 4
     cu = np.concatenate(
         [
             qu[o : o + cols, p : p + cols // 4],
             qu[o : o + cols, p - RIM : p],
             qu[o : o + cols, p + cols // 4 : p + cols // 4 + RIM],
-            np.zeros((cols, 128 - 2 * RIM)),
         ],
         1,
     ).T
-    ru_own = split_const(qu[o : o + rows, p : p + rows // 4])
-    above_part, below_part = qu[o : o + rows, p - RIM : p], qu[o : o + rows, p + rows // 4 : p + rows // 4 + RIM]
-    assert not above_part[BAND_ROWS:].any() and not below_part[: rows - BAND_ROWS].any()
-    nothing = np.zeros((BAND_ROWS, RIM))
-    ru_rim = split_const(
-        np.block([[above_part[:BAND_ROWS], nothing], [nothing, below_part[rows - BAND_ROWS :]]])
-    )
-    three = lambda pair: np.concatenate([pair[0], pair[0], pair[1]], 1)
+    ru = qu[o : o + rows]
+    ru_own, ru_rims = ru[:, p : p + low], (ru[:, p - RIM : p], ru[:, p + low : p + low + RIM])
+    ru_ends = (ru_rims[0][:BAND_ROWS], ru_rims[1][rows - BAND_ROWS :])
+    assert not ru_rims[0][BAND_ROWS:].any() and not ru_rims[1][: rows - BAND_ROWS].any()
+
+    def three(m):
+        hi, lo = split_const(m)
+        return np.concatenate([hi, hi, lo], 1)
+
     pair = lambda m: np.concatenate(split_const(m), 1)
-    parts = dict(
-        below=pair(below),
-        above=pair(above),
-        own=pair(np.concatenate(own)),
-        ru_own=three(ru_own),
-        ru_rim=three(ru_rim),
-    )
+    parts = dict(below=pair(below), above=pair(above))
+    for side in range(2):
+        parts[f"edge{side}"] = np.concatenate([three(m) for m in edge[side]])
+    for side in range(2):
+        parts[f"ru{side}"] = three(np.concatenate([ru_own, ru_rims[side]], 1))
+    for side in range(2):
+        parts[f"end{side}"] = three(ru_ends[side])
     for level in range(LEVELS):
-        parts[f"edge{level}"] = edge[level]
+        parts[f"own{level}"] = pair(own[level])
         parts[f"c1{level}hi"], parts[f"c1{level}lo"] = split_const(c1[level])
         for h in range(2):
             parts[f"c2{level}{h}hi"], parts[f"c2{level}{h}lo"] = split_const(c2[level][h])
@@ -145,8 +141,7 @@
         where[name] = (at, m.shape)
         at += high
     table = np.concatenate(table).astype(BF16)
-    count = where["own"][0]
-    return table, table[:count], where
+    return table, table[: where["edge0"][0]], where
 
 
 class Table:
@@ -161,6 +156,11 @@
         x = self[name]
         wide = x.shape[1] // 2
         return x[:, :wide], x[:, wide:]
+
+    def side(self, name, below):
+        (first, (high, wide)), (second, _) = self.where[name + "0"], self.where[name + "1"]
+        at = pl.multiple_of(jnp.where(below, second, first), 16)
+        return self.ref[pl.ds(at, high), 0:wide]
 
     def two(self, name):
         return self[name + "hi"], self[name + "lo"]
@@ -204,6 +204,20 @@
     return dot(a[0], b[0], dims) + dot(a[1], b[0], dims) + dot(a[0], b[1], dims)
 
 
+def rows3(a, b):
+    high = a[0].shape[0]
+    both = dot(jnp.concatenate(a, 0), b[0])
+    return both[:high] + both[high:] + dot(a[0], b[1])
+
+
+def three_high(x):
+    if x.shape[0] % 16:
+        hi = x.astype(BF16).astype(F32)
+        return jnp.concatenate([hi, x - hi, hi], 0).astype(BF16)
+    hi, lo = split(x)
+    return jnp.concatenate([hi, lo, hi], 0)
+
+
 def lanes(shape):
     return lax.broadcasted_iota(jnp.int32, shape, 1)
 
@@ -239,7 +253,20 @@
             out[main + RIM : main + RIM + COEFS, :] = dot3(v, split(edge[:, :REACH]), ((1,), (1,)))
 
 
-def stage_kernel(count, where, ms_ref, pan_ref, table_ref, own_ref, top_ref, bot_ref):
+def stage_kernel(count, where, first, *refs):
+    ms_hbm, pan_hbm, table_hbm, own_ref, top_ref, bot_ref, pan_ref, table_ref, ms_ref, sems = refs
+    rest = table_ref.shape[0] - first
+    moves = [
+        (table_hbm.at[pl.ds(0, first)], table_ref.at[pl.ds(0, first)]),
+        (pan_hbm, pan_ref),
+        (ms_hbm, ms_ref),
+        (table_hbm.at[pl.ds(first, rest)], table_ref.at[pl.ds(first, rest)]),
+    ]
+    copies = [pltpu.make_async_copy(x, y, sems.at[k]) for k, (x, y) in enumerate(moves)]
+    for copy in copies:
+        copy.start()
+    for copy in copies[:3]:
+        copy.wait()
     table = Table(table_ref, where)
     pack_chunk(own_ref, ms_ref, lax.axis_index("col"), count)
     rows = pan_ref.shape[0]
@@ -247,6 +274,7 @@
         full = dot3(table.pair(name), split(pan_ref[at : at + REACH, :]))
         for k in range(pan_ref.shape[1] // 128):
             out[k * COEFS : (k + 1) * COEFS, :] = full[:, k * 128 : (k + 1) * 128]
+    copies[3].wait()
 
 
 def rim_kernel(count, low, where, top_ref, bot_ref, table_ref, *refs):
@@ -307,60 +335,93 @@
     )
 
 
-def columns(t, cols, table, level):
+def columns(x, cols, table, level):
     half = cols // 2
+    high = x.shape[0]
+    wide = 2 * COEFS + REACH
+    main = rows3(split(jnp.concatenate([x[:, :half], x[:, half:cols]], 0)), table.two(f"c1{level}"))
     out = []
     for h in range(2):
-        own = tuple(x[:, h * half : (h + 1) * half] for x in t)
-        rim = tuple(x[:, cols + h * 128 : cols + (h + 1) * 128] for x in t)
-        out.append(
-            dot3(own, table.two(f"c1{level}")) + dot3(rim, table.two(f"c2{level}{h}"))
-        )
+        rim = split(x[:, cols + h * 128 : cols + h * 128 + wide])
+        product = dot3 if high % 16 else rows3
+        out.append(main[h * high : (h + 1) * high] + product(rim, table.two(f"c2{level}{h}")))
     return out
 
 
-def low_columns(x, table):
-    return jnp.concatenate([dot3(x, table.two(f"cu{h}")) for h in range(2)], 1)
+def low_columns(x_ref, y_ref, table):
+    x = split(x_ref[:, 0 : 128 + 2 * RIM])
+    half = y_ref.shape[1] // 2
+    for h in range(2):
+        y_ref[:, h * half : (h + 1) * half] = rows3(x, table.two(f"cu{h}"))
+
+
+def fill_rows(xe, at, cols, piece, xh):
+    blocks = cols // 128
+    for k in range(blocks):
+        xe[at, k * 128 : (k + 1) * 128] = piece(k)
+    f, s = own_rims(piece(blocks // 2), piece(blocks // 2 - 1), xh)
+    xe[at, cols : cols + 128] = f
+    xe[at, cols + 128 : cols + 256] = s
+
+
+def coef_piece(ref):
+    return lambda k: ref[k * COEFS : (k + 1) * COEFS, :]
+
+
+def band_rims(mext, ref, total, base, high, skip):
+    for n in range(total):
+        at = slice(n * high + skip, n * high + skip + RIM)
+        mext[at, 0:128] = ref[base + n * RIM : base + (n + 1) * RIM, :]
+        spot = base + total * RIM + (n // 4) * RIM
+        mext[at, 128:256] = pltpu.roll(ref[spot : spot + RIM, :], (-2 * RIM * (n % 4)) % 128, 1)
 
 
 def local_kernel(count, low, where, gains_ref, *refs):
     q, refs = refs[:count], refs[count:]
-    pan_ref, xh_ref, table_ref, part_ref, xe, e3, mext = refs
+    pan_ref, xh_ref, a_ref, table_ref, part_ref, gains_out, xe, tr, e3, mext, y_ref = refs
     table = Table(table_ref, where)
-    c = lax.axis_index("col")
+    c, r = lax.axis_index("col"), lax.axis_index("row")
+    below = lax.rem(r, 2) == 0
     steps = column_steps(count)
     bands = (q[0].shape[0] - RIM) // low
+    total = count * bands
     main = bands * low
     rows, cols = pan_ref.shape
     half = cols // 2
-    xe[:, 0:cols] = pan_ref[...]
-    f, s = own_rims(pan_ref[:, half : half + 128], pan_ref[:, half - 128 : half], xh_ref[...])
-    xe[:, cols : cols + 128] = f
-    xe[:, cols + 128 : cols + 256] = s
-    x = split(xe[...])
-    for level in range(LEVELS):
-        rs = slice(level * rows, (level + 1) * rows)
-        t = split(dot3(tuple(m[rs] for m in table.pair("own")), x))
-        for h, e in enumerate(columns(t, cols, table, level)):
-            e3[level, :, h * half : (h + 1) * half] = e
     per = low // RIM
-    for n in range(count * bands):
+    high = low + RIM
+    for n in range(total):
         ref, i = q[n // bands], n % bands
-        mext[n * low : (n + 1) * low, 0:128] = ref[i * low : (i + 1) * low, :]
+        mext[n * high : n * high + low, 0:128] = ref[i * low : (i + 1) * low, :]
         for g in range(per):
-            at = n * low + g * RIM
+            at = n * high + g * RIM
             mext[at : at + RIM, 128:256] = pltpu.roll(
                 ref[main : main + RIM, :], (-2 * RIM * (i * per + g)) % 128, 1
             )
+    band_rims(mext, a_ref, total, (cols // 128 + 1) * COEFS, high, low)
+    low_columns(mext, y_ref, table)
+    fill_rows(xe, slice(0, rows), cols, lambda k: pan_ref[:, k * 128 : (k + 1) * 128], xh_ref[...])
+    fill_rows(xe, slice(rows, rows + COEFS), cols, coef_piece(a_ref), a_ref[cols // 128 * COEFS : (cols // 128 + 1) * COEFS, :])
+    hi, lo = split(xe[0:rows, :])
+    both = jnp.concatenate([hi, lo], 0)
+    added = dot(table.side("edge", below), three_high(xe[rows : rows + COEFS, :]))
+    for level in range(LEVELS):
+        ohi, olo = table.pair(f"own{level}")
+        tr[level] = dot(jnp.concatenate([ohi, ohi], 1), both) + dot(olo, hi)
+        at = pl.ds(pl.multiple_of(jnp.where(below, rows - REACH, 0), 16), REACH)
+        tr[level, at, :] = tr[level, at, :] + added[level * REACH : (level + 1) * REACH]
+        for h, e in enumerate(columns(tr[level], cols, table, level)):
+            e3[level, :, h * half : (h + 1) * half] = e
     for j in range(count):
         src = c if j == 0 else steps[j - 1][3](c)
-        y = low_columns(split(mext[j * main : (j + 1) * main, :]), table)
         for i in range(bands):
+            n = j * bands + i
             band = src * bands + i
-            hi, lo = split(y[i * low : (i + 1) * low])
             g1, g2, g3 = gains_ref[band, 0], gains_ref[band, 1], gains_ref[band, 2]
-            part_ref[j * bands + i] = (
-                dot(table["ru_own"], jnp.concatenate([hi, lo, hi], 0))
+            for k, g in enumerate((g2 - g1, g3 - g2, -g3)):
+                gains_out[3 * n + k : 3 * n + k + 1, :] = jnp.full((1, cols), g, F32)
+            part_ref[n] = (
+                dot(table.side("ru", below), three_high(y_ref[n * high : (n + 1) * high, :]))
                 + g1 * pan_ref[...]
                 + (g2 - g1) * e3[0]
                 + (g3 - g2) * e3[1]
@@ -368,59 +429,47 @@
             )
 
 
-def main_kernel(count, low, bands, where, gains_ref, *refs):
-    part_ref, a_ref, b_ref, table_ref, out_ref, xe, de, mext, obuf, sems = refs
+def main_kernel(count, low, bands, where, *refs):
+    part_ref, gains_ref, b_ref, table_ref, out_ref, xe, de, mext, y_ref, obuf, sems = refs
     table = Table(table_ref, where)
     c, r = lax.axis_index("col"), lax.axis_index("row")
     steps = column_steps(count)
-    even = lax.rem(r, 2) == 0
+    below = lax.rem(r, 2) == 1
     total, rows, cols = part_ref.shape
     half = cols // 2
     blocks = cols // 128
-    mid = half // 128
-    base = (blocks + 1) * COEFS
-    for ref, below in ((a_ref, even), (b_ref, jnp.logical_not(even))):
-        at = pl.ds(pl.multiple_of(jnp.where(below, COEFS, 0), 8), COEFS)
-        piece = lambda k: ref[k * COEFS : (k + 1) * COEFS, :]
-        for k in range(blocks):
-            xe[at, k * 128 : (k + 1) * 128] = piece(k)
-        f, s = own_rims(piece(mid), piece(mid - 1), piece(blocks))
-        xe[at, cols : cols + 128] = f
-        xe[at, cols + 128 : cols + 256] = s
-        for n in range(total):
-            at = pl.ds(pl.multiple_of(n * 2 * RIM + jnp.where(below, RIM, 0), 16), RIM)
-            mext[at, 0:128] = ref[base + n * RIM : base + (n + 1) * RIM, :]
-            spot = base + total * RIM + (n // 4) * RIM
-            mext[at, 128:256] = pltpu.roll(ref[spot : spot + RIM, :], (-2 * RIM * (n % 4)) % 128, 1)
-    x = split(xe[...])
+    source = [c if j == 0 else steps[j - 1][3](c) for j in range(count)]
+    band = [source[n // bands] * bands + n % bands for n in range(total)]
+    done = pl.ds(pl.multiple_of(jnp.where(below, 0, BAND_ROWS), 8), rows - BAND_ROWS)
+    late = pl.ds(pl.multiple_of(jnp.where(below, rows - BAND_ROWS, 0), 8), BAND_ROWS)
+    copies = [
+        pltpu.make_async_copy(part_ref.at[n, done], out_ref.at[band[n], done], sems.at[0, n])
+        for n in range(total)
+    ]
+    for copy in copies:
+        copy.start()
+    band_rims(mext, b_ref, total, (blocks + 1) * COEFS, RIM, 0)
+    low_columns(mext, y_ref, table)
+    fill_rows(xe, slice(0, COEFS), cols, coef_piece(b_ref), b_ref[blocks * COEFS : (blocks + 1) * COEFS, :])
+    edges = table.side("edge", below)
+    gap = BAND_ROWS - REACH
+    de[:, pl.ds(pl.multiple_of(jnp.where(below, 0, REACH), 8), gap), :] = jnp.zeros((LEVELS, gap, cols), F32)
+    at = pl.ds(pl.multiple_of(jnp.where(below, gap, 0), 8), REACH)
     for level in range(LEVELS):
-        for h, z in enumerate(columns(x, cols, table, level)):
-            hi, lo = split(z)
-            de[level, :, h * half : (h + 1) * half] = dot(table[f"edge{level}"], jnp.concatenate([hi, lo, hi], 0))
-    copies = []
-    for j in range(count):
-        src = c if j == 0 else steps[j - 1][3](c)
-        high = bands * 2 * RIM
-        y = low_columns(split(mext[j * high : (j + 1) * high, :]), table)
-        for i in range(bands):
-            band = src * bands + i
-            n = j * bands + i
-            hi, lo = split(y[i * 2 * RIM : (i + 1) * 2 * RIM])
-            g1, g2, g3 = gains_ref[band, 0], gains_ref[band, 1], gains_ref[band, 2]
-            add = dot(table["ru_rim"], jnp.concatenate([hi, lo, hi], 0))
-            fix = (g2 - g1) * de[0] + (g3 - g2) * de[1] - g3 * de[2]
-            top = add[:BAND_ROWS]
-            top = jnp.concatenate([top[:REACH] + fix[:REACH], top[REACH:]], 0)
-            low_end = add[BAND_ROWS:]
-            low_end = jnp.concatenate(
-                [low_end[: BAND_ROWS - REACH], low_end[BAND_ROWS - REACH :] + fix[REACH:]], 0
-            )
-            obuf[n, 0:BAND_ROWS] = part_ref[n, 0:BAND_ROWS] + top
-            obuf[n, BAND_ROWS : rows - BAND_ROWS] = part_ref[n, BAND_ROWS : rows - BAND_ROWS]
-            obuf[n, rows - BAND_ROWS :] = part_ref[n, rows - BAND_ROWS :] + low_end
-            copy = pltpu.make_async_copy(obuf.at[n], out_ref.at[band], sems.at[n])
-            copy.start()
-            copies.append(copy)
+        for h, z in enumerate(columns(xe[...], cols, table, level)):
+            de[level, at, h * half : (h + 1) * half] = dot(edges[level * REACH : (level + 1) * REACH], three_high(z))
+    for n in range(total):
+        g = [gains_ref[3 * n + k : 3 * n + k + 1, :] for k in range(LEVELS)]
+        obuf[n] = (
+            part_ref[n, late, :]
+            + dot(table.side("end", below), three_high(y_ref[n * RIM : (n + 1) * RIM, :]))
+            + g[0] * de[0]
+            + g[1] * de[1]
+            + g[2] * de[2]
+        )
+        copy = pltpu.make_async_copy(obuf.at[n], out_ref.at[band[n], late], sems.at[1, n])
+        copy.start()
+        copies.append(copy)
     for copy in copies:
         copy.wait()
 
@@ -439,7 +488,7 @@
     last = cols // 128 - 1
     packed = pl.pallas_call(
         functools.partial(pack_kernel, count, where),
-        out_shape=[shape(h) for h in heights],
+        out_shape=[pltpu.VMEM((h, 128), F32) for h in heights],
         grid=(1,),
         in_specs=[
             pl.BlockSpec(multispectral.shape, lambda i: (0, 0, 0)),
@@ -447,22 +496,31 @@
             pl.BlockSpec((rows, 128), lambda i: (0, last)),
             pl.BlockSpec(small.shape, lambda i: (0, 0)),
         ],
-        out_specs=[pl.BlockSpec((h, 128), lambda i: (0, 0)) for h in heights],
+        out_specs=[whole for h in heights],
         name="pack",
-    )(multispectral, panchromatic, panchromatic, jnp.asarray(small))
+    )(*(pltpu.with_memory_space_constraint(x, pltpu.HBM) for x in (multispectral, panchromatic, panchromatic, jnp.asarray(small))))
     params = lambda mib: pltpu.CompilerParams(vmem_limit_bytes=mib << 20)
     cost = lambda flops: pl.CostEstimate(flops=flops, bytes_accessed=10**6, transcendentals=0)
     table = jnp.asarray(table)
     height = cols // 128 * COEFS
-    own, top, bot = pl.pallas_call(
-        functools.partial(stage_kernel, count, where),
-        out_shape=[shape(chunk), shape(height), shape(height)],
-        in_specs=[whole] * 3,
-        out_specs=[whole] * 3,
+    first = small.shape[0]
+    in_hbm = lambda *xs: [pltpu.with_memory_space_constraint(x, pltpu.HBM) for x in xs]
+    own, top, bot, pan, table = pl.pallas_call(
+        functools.partial(stage_kernel, count, where, first),
+        out_shape=[
+            VMEM((chunk, 128), F32),
+            VMEM((height, 128), F32),
+            VMEM((height, 128), F32),
+            VMEM((rows, cols), F32),
+            VMEM(table.shape, BF16),
+        ],
+        in_specs=[pl.BlockSpec(memory_space=pltpu.HBM)] * 3,
+        out_specs=[whole] * 5,
+        scratch_shapes=[VMEM(multispectral.shape, F32), pltpu.SemaphoreType.DMA((4,))],
         compiler_params=params(8),
         cost_estimate=cost(10**9),
         name="stage",
-    )(multispectral, panchromatic, table)
+    )(*in_hbm(multispectral, panchromatic, table))
     q = [own] + [lax.ppermute(x, "col", step[0]) for x, step in zip(packed, steps)]
     sent = height + COEFS + total * RIM + -(-total // 4) * RIM
     a, b, xh = pl.pallas_call(
@@ -476,35 +534,38 @@
     a = lax.ppermute(a, "row", swap_pairs(row_count))
     b = lax.ppermute(b, "row", odd_pairs(row_count))
     smem = pl.BlockSpec(memory_space=pltpu.SMEM)
-    part = pl.pallas_call(
+    part, scaled = pl.pallas_call(
         functools.partial(local_kernel, count, low, where),
-        out_shape=jax.ShapeDtypeStruct((total, rows, cols), F32),
-        in_specs=[smem] + [whole] * (count + 3),
-        out_specs=whole,
+        out_shape=[jax.ShapeDtypeStruct((total, rows, cols), F32), shape(LEVELS * total, cols)],
+        in_specs=[smem] + [whole] * (count + 4),
+        out_specs=[whole] * 2,
         scratch_shapes=[
-            VMEM((rows, cols + 256), F32),
+            VMEM((rows + COEFS, cols + 256), F32),
+            VMEM((LEVELS, rows, cols + 256), F32),
             VMEM((LEVELS, rows, cols), F32),
-            VMEM((total * low, 256), F32),
+            VMEM((total * (low + RIM), 256), F32),
+            VMEM((total * (low + RIM), cols), F32),
         ],
         compiler_params=params(16),
         cost_estimate=cost(4 * 10**9),
         name="local",
-    )(band_gains, *q, panchromatic, xh, table)
+    )(band_gains, *q, pan, xh, a, table)
     return pl.pallas_call(
         functools.partial(main_kernel, count, low, bands, where),
         out_shape=jax.ShapeDtypeStruct((total, rows, cols), F32),
-        in_specs=[smem] + [whole] * 4,
+        in_specs=[whole] * 4,
         out_specs=pl.BlockSpec(memory_space=pltpu.HBM),
         scratch_shapes=[
-            VMEM((2 * COEFS, cols + 256), F32),
-            VMEM((LEVELS, 2 * REACH, cols), F32),
-            VMEM((total * 2 * RIM, 256), F32),
-            VMEM((total, rows, cols), F32),
-            pltpu.SemaphoreType.DMA((total,)),
+            VMEM((COEFS, cols + 256), F32),
+            VMEM((LEVELS, BAND_ROWS, cols), F32),
+            VMEM((total * RIM, 256), F32),
+            VMEM((total * RIM, cols), F32),
+            VMEM((total, BAND_ROWS, cols), F32),
+            pltpu.SemaphoreType.DMA((2, total)),
         ],
         compiler_params=params(16),
         name="combine",
-    )(band_gains, part, a, b, table)
+    )(part, scaled, b, table)
 
 
 def solution(mesh):

time: 24.4 us -> 21.9 us (0.90)
  local copies, waits for them, and re-layouts: 3.68 us -> 0.09 us
  waiting for transfers between devices: 2.25 us -> 4.78 us
  Pallas kernels: 10 us -> 8.63 us
    unnamed x13 -> x3, local copies, waits for them, and re-layouts: 3.68 us -> 0.09 us
    ppermute x3, waiting for transfers between devices: 2.22 us -> 4.06 us  [on_device(): lax.ppermute(x, 'col', step[0])]
    pallas_call x1, Pallas kernels: 3.89 us -> 2.33 us  [on_device(): pl.pallas_call(functools.partial(main_kernel, count, low, bands, where),...]
    pallas_call x2, Pallas kernels: 2.12 us -> 3.09 us  [the longest x1 1.86 us: on_device(): pl.pallas_call(functools.partial(stage_kernel, count, where, first), out_...]
    pallas_call x1, Pallas kernels: 3.75 us -> 2.96 us  [on_device(): pl.pallas_call(functools.partial(local_kernel, count, low, where), out_sh...]
    ppermute x1, waiting for transfers between devices: 0.03 us -> 0.72 us  [on_device(): b = lax.ppermute(b, 'row', odd_pairs(row_count))]
  transfers between devices with their start and end apart: 5 -> 5, of which waited for: 1 -> 3; matrix products, arithmetic and copies ran while one was open for 0% -> 0% of each run, Pallas kernels for 16% -> 22%
where the time goes in v1:
time: 21.9 us; the launch traced here: 21.7 us
  Pallas kernels  8.63 us (39%)
  starting transfers between devices  8.2 us (37%)
  waiting for transfers between devices  4.78 us (22%)
    ppermute x3, starting transfers between devices, on_device(): lax.ppermute(x, 'col', step[0])  5.65 us
    ppermute x3, waiting for transfers between devices, on_device(): lax.ppermute(x, 'col', step[0])  4.06 us
    pallas_call x1, Pallas kernels, on_device(): pl.pallas_call(functools.partial(local_kernel, count, low, where), out_sh...  2.96 us
    ppermute x1, starting transfers between devices, on_device(): b = lax.ppermute(b, 'row', odd_pairs(row_count))  2.54 us
    pallas_call x1, Pallas kernels, on_device(): pl.pallas_call(functools.partial(main_kernel, count, low, bands, where),...  2.33 us
    pallas_call x1, Pallas kernels, on_device(): pl.pallas_call(functools.partial(stage_kernel, count, where, first), out_...  1.86 us
    pallas_call x1, Pallas kernels, on_device(): pl.pallas_call(functools.partial(pack_kernel, count, where), out_shape=[p...  1.23 us
    ppermute x1, waiting for transfers between devices, on_device(): b = lax.ppermute(b, 'row', odd_pairs(row_count))  0.72 us
  transfers between devices with their start and end apart: 5, of which 3 were waited for; matrix products, arithmetic and copies ran while one was open for 0% of the time, Pallas kernels for 22%

profile of v1, /device:TPU:0, one launch (start us, length us, event | category | flops | bytes accessed | tf_op | source)
XLA Modules:
  0.0 21.7 jit_solution(9912398325152056584)
XLA Ops:
  0.0 1.2 %pack.1 = (f32[104,128]{1,0:T(8,128)S(1)}, f32[104,128]{1,0:T(8,128)S(1)}, f32[80,128]{1,0:T(8,128)S(1)}) custom-call(f32[2,32,512]{2,1,0:T(8,128)} %ms_ref.1, f32[128,512]{1,0:T(8,128)} %last_ref.1, f32[128,512]{1,0:T(8,128)} %last_ref.1, bf16[64,256]{1,0:T(8,128)(2,1)} %constant.4.clone.table_ref), custom_call_target="tpu_custom_call" | custom-call | tf_op jit(solution)/shard_map/pack/pallas_call | solution.py:489
  1.2 4.1 %collective-permute-start.2 = (f32[80,128]{1,0:T(8,128)S(1)}, f32[80,128]{1,0:T(8,128)S(1)}, u32[]{:S(2)}, u32[]{:S(2)}) collective-permute-start(f32[80,128]{1,0:T(8,128)S(1)} %get-tuple-element.21), channel_id=1, source_target_pairs={{0,2},{1,3},{2,0},{3,1},{4,6},{5,7},{6,4},{7,5},{8,10},{9,11},{10,... | collective-permute-start | bytes 122888 | tf_op jit(solution)/shard_map/ppermute | solution.py:524
  5.3 1.6 %collective-permute-start = (f32[104,128]{1,0:T(8,128)S(1)}, f32[104,128]{1,0:T(8,128)S(1)}, u32[]{:S(2)}, u32[]{:S(2)}) collective-permute-start(f32[104,128]{1,0:T(8,128)S(1)} %get-tuple-element.19), channel_id=1, source_target_pairs={{0,1},{1,0},{2,3},{3,2},{4,5},{5,4},{6,7},{7,6},{8,9},{9,8},{10,11... | collective-permute-start | bytes 159752 | tf_op jit(solution)/shard_map/ppermute | solution.py:524
  6.9 0.0 copy-start
  6.9 0.0 collective-permute-start.1
  6.9 1.9 %stage.1 = (f32[80,128]{1,0:T(8,128)S(1)}, f32[96,128]{1,0:T(8,128)S(1)}, f32[96,128]{1,0:T(8,128)S(1)}, f32[128,512]{1,0:T(8,128)S(1)}, bf16[4448,256]{1,0:T(8,128)(2,1)S(1)}) custom-call(f32[2,32,512]{2,1,0:T(8,128)} %ms_ref.1, f32[128,512]{1,0:T(8,128)} %last_ref.1, bf16[4448,256]{1,0:T(8,128)(2,1)} %constant.5.clone.refs_2_), custom_call_target="tpu_custom_call" | custom-call | flops 1000000000 | bytes 1000000 | tf_op jit(solution)/shard_map/stage/pallas_call | solution.py:508
  8.7 0.0 collective-permute-done.2.refs_3_
  8.8 0.7 %collective-permute-done.refs_1_ = f32[104,128]{1,0:T(8,128)S(1)} collective-permute-done((f32[104,128]{1,0:T(8,128)S(1)}, f32[104,128]{1,0:T(8,128)S(1)}, u32[]{:S(2)}, u32[]{:S(2)}) %collective-permute-start) | collective-permute-done | bytes 53280 | tf_op jit(solution)/shard_map/ppermute | solution.py:524
  9.4 3.4 %collective-permute-done.1.refs_2_ = f32[104,128]{1,0:T(8,128)S(1)} collective-permute-done((f32[104,128]{1,0:T(8,128)S(1)}, f32[104,128]{1,0:T(8,128)S(1)}, u32[]{:S(2)}, u32[]{:S(2)}) %collective-permute-start.1) | collective-permute-done | bytes 53280 | tf_op jit(solution)/shard_map/ppermute | solution.py:524
  12.8 0.3 %rim.1 = (f32[280,128]{1,0:T(8,128)S(1)}, f32[280,128]{1,0:T(8,128)S(1)}, f32[128,128]{1,0:T(8,128)S(1)}) custom-call(f32[96,128]{1,0:T(8,128)S(1)} %get-tuple-element.23.top_ref, f32[96,128]{1,0:T(8,128)S(1)} %get-tuple-element.24.bot_ref, bf16[4448,256]{1,0:T(8,128)(2,1)S(1)} %get-tuple-element.25.table_ref.refs_7_.refs_3_, ...), custom_call_target="tpu_custom_call" | custom-call | tf_op jit(solution)/shard_map/rim/pallas_call | solution.py:526
  13.1 0.0 collective-permute-start.3
  13.1 0.0 copy-done
  13.1 0.1 copy.6.gains_ref
  13.2 2.5 %collective-permute-start.4 = (f32[280,128]{1,0:T(8,128)S(1)}, f32[280,128]{1,0:T(8,128)S(1)}, u32[]{:S(2)}, u32[]{:S(2)}) collective-permute-start(f32[280,128]{1,0:T(8,128)S(1)} %get-tuple-element.30), channel_id=1, source_target_pairs={{0,28},{4,8},{8,4},{12,16},{16,12},{20,24},{24,20},{28,0},{1,29},{... | collective-permute-start | bytes 430088 | tf_op jit(solution)/shard_map/ppermute | solution.py:535
  15.7 0.0 collective-permute-done.3.refs_6_
  15.7 3.0 %local.1 = (f32[8,128,512]{2,1,0:T(8,128)S(1)}, f32[24,512]{1,0:T(8,128)S(1)}) custom-call(f32[8,3]{1,0:T(8,128)S(1)} %copy.6.gains_ref, f32[80,128]{1,0:T(8,128)S(1)} %get-tuple-element.18.refs_0_, f32[104,128]{1,0:T(8,128)S(1)} %collective-permute-done.refs_1_, f32[104,128]{1,0:T(8,128)S(1)} %collective-permute-done.1.refs_2_, ...), custom_call_target="tpu_custom_call" | custom-call | flops 4000000000 | bytes 1000000 | tf_op jit(solution)/shard_map/local/pallas_call | solution.py:537
  18.7 0.7 %collective-permute-done.4.refs_2_ = f32[280,128]{1,0:T(8,128)S(1)} collective-permute-done((f32[280,128]{1,0:T(8,128)S(1)}, f32[280,128]{1,0:T(8,128)S(1)}, u32[]{:S(2)}, u32[]{:S(2)}) %collective-permute-start.4) | collective-permute-done | bytes 143392 | tf_op jit(solution)/shard_map/ppermute | solution.py:535
  19.4 2.3 %combine.1 = f32[8,128,512]{2,1,0:T(8,128)} custom-call(f32[8,128,512]{2,1,0:T(8,128)S(1)} %get-tuple-element.28.refs_0_, f32[24,512]{1,0:T(8,128)S(1)} %get-tuple-element.29.refs_1_, f32[280,128]{1,0:T(8,128)S(1)} %collective-permute-done.4.refs_2_, bf16[4448,256]{1,0:T(8,128)(2,1)S(1)} %get-tuple-element.25.table_ref.refs_7_.refs_3_), custom_call_target="tpu_custom_call" | custom-call | tf_op jit(solution)/shard_map/combine/pallas_call | solution.py:553
Async XLA Ops:
  1.2 7.5 %collective-permute-start.2 = (f32[80,128]{1,0:T(8,128)S(1)}, f32[80,128]{1,0:T(8,128)S(1)}, u32[]{:S(2)}, u32[]{:S(2)}) collective-permute-start(f32[80,128]{1,0:T(8,128)S(1)} %get-tuple-element.21), channel_id=1, source_target_pairs={{0,2},{1,3},{2,0},{3,1},{4,6},{5,7},{6,4},{7,5},{8,10},{9,11},{10,... | collective-permute-start | bytes 122888 | tf_op jit(solution)/shard_map/ppermute | solution.py:524
  5.3 4.1 %collective-permute-start = (f32[104,128]{1,0:T(8,128)S(1)}, f32[104,128]{1,0:T(8,128)S(1)}, u32[]{:S(2)}, u32[]{:S(2)}) collective-permute-start(f32[104,128]{1,0:T(8,128)S(1)} %get-tuple-element.19), channel_id=1, source_target_pairs={{0,1},{1,0},{2,3},{3,2},{4,5},{5,4},{6,7},{7,6},{8,9},{9,8},{10,11... | collective-permute-start | bytes 159752 | tf_op jit(solution)/shard_map/ppermute | solution.py:524
  6.9 6.2 %copy-start = (f32[8,3]{0,1:T(4,128)S(1)}, f32[8,3]{0,1:T(4,128)}, u32[]{:S(2)}) copy-start(f32[8,3]{0,1:T(4,128)} %param.7) | copy-start | bytes 292
  6.9 5.9 %collective-permute-start.1 = (f32[104,128]{1,0:T(8,128)S(1)}, f32[104,128]{1,0:T(8,128)S(1)}, u32[]{:S(2)}, u32[]{:S(2)}) collective-permute-start(f32[104,128]{1,0:T(8,128)S(1)} %get-tuple-element.20), channel_id=1, source_target_pairs={{0,3},{1,2},{2,1},{3,0},{4,7},{5,6},{6,5},{7,4},{8,11},{9,10},{10,... | collective-permute-start | bytes 159752 | tf_op jit(solution)/shard_map/ppermute | solution.py:524
  13.1 2.7 %collective-permute-start.3 = (f32[280,128]{1,0:T(8,128)S(1)}, f32[280,128]{1,0:T(8,128)S(1)}, u32[]{:S(2)}, u32[]{:S(2)}) collective-permute-start(f32[280,128]{1,0:T(8,128)S(1)} %get-tuple-element.27), channel_id=1, source_target_pairs={{0,4},{4,0},{8,12},{12,8},{16,20},{20,16},{24,28},{28,24},{1,5},{5... | collective-permute-start | bytes 430088 | tf_op jit(solution)/shard_map/ppermute | solution.py:534
  13.2 6.2 %collective-permute-start.4 = (f32[280,128]{1,0:T(8,128)S(1)}, f32[280,128]{1,0:T(8,128)S(1)}, u32[]{:S(2)}, u32[]{:S(2)}) collective-permute-start(f32[280,128]{1,0:T(8,128)S(1)} %get-tuple-element.30), channel_id=1, source_target_pairs={{0,28},{4,8},{8,4},{12,16},{16,12},{20,24},{24,20},{28,0},{1,29},{... | collective-permute-start | bytes 430088 | tf_op jit(solution)/shard_map/ppermute | solution.py:535

commit v2 on v1

--- a/solution.py
+++ b/solution.py
@@ -22,6 +22,8 @@
 REACH = 48
 COEFS = 24
 RIM = 16
+NEED = 13
+RANK = 21
 BAND_ROWS = 56
 VMEM = pltpu.VMEM
 F32, BF16 = jnp.float32, jnp.bfloat16
@@ -78,8 +80,8 @@
     o = 256
     stack = lambda lo, hi: np.concatenate([m[o : o + 128, lo:hi] for m in q])
     send, recv = [], []
-    for lo, hi, base in ((o - REACH, o, 0), (o + 128, o + 128 + REACH, 0)):
-        u, s, vt = np.linalg.svd(stack(lo, hi), full_matrices=False)
+    for lo, hi in ((o - REACH, o), (o + 128, o + 128 + REACH)):
+        _, s, vt = np.linalg.svd(stack(lo, hi), full_matrices=False)
         assert s[COEFS - 3] < 1e-14
         send.append(vt[:COEFS])
         recv.append(vt[:COEFS].T)
@@ -126,7 +128,13 @@
     for side in range(2):
         parts[f"ru{side}"] = three(np.concatenate([ru_own, ru_rims[side]], 1))
     for side in range(2):
-        parts[f"end{side}"] = three(ru_ends[side])
+        assert not (ru_rims[0][:, : RIM - NEED] if side == 0 else ru_rims[1][:, NEED:]).any()
+        used = ru_ends[side][:, RIM - NEED :] if side == 0 else ru_ends[side][:, :NEED]
+        parts[f"end{side}"] = three(np.pad(used, ((0, 0), (0, RIM - NEED))))
+        gap = np.zeros((BAND_ROWS - REACH, COEFS))
+        for level in range(LEVELS):
+            m = edge[side][level]
+            parts[f"fix{level}{side}"] = three(np.concatenate([m, gap] if side == 0 else [gap, m]))
     for level in range(LEVELS):
         parts[f"own{level}"] = pair(own[level])
         parts[f"c1{level}hi"], parts[f"c1{level}lo"] = split_const(c1[level])
@@ -298,33 +306,42 @@
     per = low // RIM
     total = count * bands
 
-    def fill(out, bottom):
+    def fill(out, bottom, far):
         out[0:height, :] = (bot_ref if bottom else top_ref)[...]
         v = table.pair("below" if bottom else "above")
-        edge = xh[xh.shape[0] - REACH :] if bottom else xh[:REACH]
-        out[height : height + COEFS, :] = dot3(v, split(edge))
-        base = height + COEFS
+        corner = dot3(v, split(xh[xh.shape[0] - REACH :] if bottom else xh[:REACH]))
+        if far:
+            tight = jnp.where(lanes(corner.shape) < RANK, corner, pltpu.roll(corner, 128 - (COEFS - RANK), 1))
+            packed = tight[0:8]
+            for g in (1, 2):
+                turned = pltpu.roll(tight[8 * g : 8 * g + 8], 2 * RANK * g, 1)
+                packed = jnp.where(lanes(packed.shape) >= 2 * RANK * g, turned, packed)
+            out[height : height + 8, :] = packed
+        else:
+            out[height : height + COEFS, :] = corner
+        base = height + (8 if far else COEFS)
+        rim_rows = NEED if far else RIM
         packed = None
         for n in range(total):
             ref, i = q[n // bands], n % bands
-            row = (i + 1) * low - RIM if bottom else i * low
-            out[base + n * RIM : base + (n + 1) * RIM, :] = ref[row : row + RIM, :]
+            row = (i + 1) * low - rim_rows if bottom else i * low
+            out[base + n * rim_rows : base + (n + 1) * rim_rows, :] = ref[row : row + rim_rows, :]
             slot = per * (i + 1) - 1 if bottom else per * i
             rim = pltpu.roll(ref[main : main + RIM, :], (2 * RIM * (n % 4 - slot)) % 128, 1)
             packed = rim if n % 4 == 0 else jnp.where(lanes(rim.shape) >= 2 * RIM * (n % 4), rim, packed)
             if n % 4 == 3 or n == total - 1:
-                spot = base + total * RIM + (n // 4) * RIM
-                out[spot : spot + RIM, :] = packed
+                spot = base + total * rim_rows + (n // 4) * rim_rows
+                out[spot : spot + rim_rows, :] = packed[RIM - rim_rows :] if bottom else packed[:rim_rows]
 
     @pl.when(even)
     def _():
-        fill(a_ref, 1)
-        fill(b_ref, 0)
+        fill(a_ref, 1, False)
+        fill(b_ref, 0, True)
 
     @pl.when(jnp.logical_not(even))
     def _():
-        fill(a_ref, 0)
-        fill(b_ref, 1)
+        fill(a_ref, 0, False)
+        fill(b_ref, 1, True)
 
 
 def own_rims(own_right, own_left, xh):
@@ -368,12 +385,14 @@
     return lambda k: ref[k * COEFS : (k + 1) * COEFS, :]
 
 
-def band_rims(mext, ref, total, base, high, skip):
+def band_rims(mext, ref, total, base, high, skip, rim_rows=RIM):
+    filler = [jnp.zeros((RIM - rim_rows, 128), F32)] if rim_rows < RIM else []
+    whole = lambda x: jnp.concatenate([x] + filler, 0) if filler else x
     for n in range(total):
         at = slice(n * high + skip, n * high + skip + RIM)
-        mext[at, 0:128] = ref[base + n * RIM : base + (n + 1) * RIM, :]
-        spot = base + total * RIM + (n // 4) * RIM
-        mext[at, 128:256] = pltpu.roll(ref[spot : spot + RIM, :], (-2 * RIM * (n % 4)) % 128, 1)
+        mext[at, 0:128] = whole(ref[base + n * rim_rows : base + (n + 1) * rim_rows, :])
+        spot = base + total * rim_rows + (n // 4) * rim_rows
+        mext[at, 128:256] = pltpu.roll(whole(ref[spot : spot + rim_rows, :]), (-2 * RIM * (n % 4)) % 128, 1)
 
 
 def local_kernel(count, low, where, gains_ref, *refs):
@@ -404,6 +423,7 @@
     fill_rows(xe, slice(rows, rows + COEFS), cols, coef_piece(a_ref), a_ref[cols // 128 * COEFS : (cols // 128 + 1) * COEFS, :])
     hi, lo = split(xe[0:rows, :])
     both = jnp.concatenate([hi, lo], 0)
+    before = [None, None]
     added = dot(table.side("edge", below), three_high(xe[rows : rows + COEFS, :]))
     for level in range(LEVELS):
         ohi, olo = table.pair(f"own{level}")
@@ -411,25 +431,26 @@
         at = pl.ds(pl.multiple_of(jnp.where(below, rows - REACH, 0), 16), REACH)
         tr[level, at, :] = tr[level, at, :] + added[level * REACH : (level + 1) * REACH]
         for h, e in enumerate(columns(tr[level], cols, table, level)):
-            e3[level, :, h * half : (h + 1) * half] = e
+            hs = slice(h * half, (h + 1) * half)
+            e3[level, :, hs] = (pan_ref[:, hs] if level == 0 else before[h]) - e
+            before[h] = e
     for j in range(count):
         src = c if j == 0 else steps[j - 1][3](c)
         for i in range(bands):
             n = j * bands + i
             band = src * bands + i
             g1, g2, g3 = gains_ref[band, 0], gains_ref[band, 1], gains_ref[band, 2]
-            for k, g in enumerate((g2 - g1, g3 - g2, -g3)):
+            for k, g in enumerate((g1, g2, g3)):
                 gains_out[3 * n + k : 3 * n + k + 1, :] = jnp.full((1, cols), g, F32)
             part_ref[n] = (
                 dot(table.side("ru", below), three_high(y_ref[n * high : (n + 1) * high, :]))
-                + g1 * pan_ref[...]
-                + (g2 - g1) * e3[0]
-                + (g3 - g2) * e3[1]
-                - g3 * e3[2]
+                + g1 * e3[0]
+                + g2 * e3[1]
+                + g3 * e3[2]
             )
 
 
-def main_kernel(count, low, bands, where, *refs):
+def main_kernel(count, bands, where, *refs):
     part_ref, gains_ref, b_ref, table_ref, out_ref, xe, de, mext, y_ref, obuf, sems = refs
     table = Table(table_ref, where)
     c, r = lax.axis_index("col"), lax.axis_index("row")
@@ -448,16 +469,19 @@
     ]
     for copy in copies:
         copy.start()
-    band_rims(mext, b_ref, total, (blocks + 1) * COEFS, RIM, 0)
+    height = blocks * COEFS
+    band_rims(mext, b_ref, total, height + 8, RIM, 0, NEED)
     low_columns(mext, y_ref, table)
-    fill_rows(xe, slice(0, COEFS), cols, coef_piece(b_ref), b_ref[blocks * COEFS : (blocks + 1) * COEFS, :])
-    edges = table.side("edge", below)
-    gap = BAND_ROWS - REACH
-    de[:, pl.ds(pl.multiple_of(jnp.where(below, 0, REACH), 8), gap), :] = jnp.zeros((LEVELS, gap, cols), F32)
-    at = pl.ds(pl.multiple_of(jnp.where(below, gap, 0), 8), REACH)
+    packed = b_ref[height : height + 8, :]
+    tight = jnp.concatenate([pltpu.roll(packed, (-2 * RANK * g) % 128, 1) for g in range(3)], 0)
+    corner = jnp.where(lanes(tight.shape) < COEFS, tight, pltpu.roll(tight, COEFS - RANK, 1))
+    fill_rows(xe, slice(0, COEFS), cols, coef_piece(b_ref), corner)
+    before = [None, None]
     for level in range(LEVELS):
         for h, z in enumerate(columns(xe[...], cols, table, level)):
-            de[level, at, h * half : (h + 1) * half] = dot(edges[level * REACH : (level + 1) * REACH], three_high(z))
+            fix = dot(table.side(f"fix{level}", below), three_high(z))
+            de[level, :, h * half : (h + 1) * half] = -fix if level == 0 else before[h] - fix
+            before[h] = fix
     for n in range(total):
         g = [gains_ref[3 * n + k : 3 * n + k + 1, :] for k in range(LEVELS)]
         obuf[n] = (
@@ -521,11 +545,13 @@
         cost_estimate=cost(10**9),
         name="stage",
     )(*in_hbm(multispectral, panchromatic, table))
-    q = [own] + [lax.ppermute(x, "col", step[0]) for x, step in zip(packed, steps)]
-    sent = height + COEFS + total * RIM + -(-total // 4) * RIM
+    q = [own]
+    for x, step in zip(packed, steps):
+        q.append(lax.ppermute(x, "col", step[0]))
+    sent = lambda corner, rim: height + corner + total * rim + -(-total // 4) * rim
     a, b, xh = pl.pallas_call(
         functools.partial(rim_kernel, count, low, where),
-        out_shape=[shape(sent), shape(sent), shape(rows)],
+        out_shape=[shape(sent(COEFS, RIM)), shape(sent(8, NEED)), shape(rows)],
         in_specs=[whole] * (3 + count),
         out_specs=[whole] * 3,
         compiler_params=params(8),
@@ -551,7 +577,7 @@
         name="local",
     )(band_gains, *q, pan, xh, a, table)
     return pl.pallas_call(
-        functools.partial(main_kernel, count, low, bands, where),
+        functools.partial(main_kernel, count, bands, where),
         out_shape=jax.ShapeDtypeStruct((total, rows, cols), F32),
         in_specs=[whole] * 4,
         out_specs=pl.BlockSpec(memory_space=pltpu.HBM),

time: 21.9 us -> 21.6 us (0.986)
  waiting for transfers between devices: 4.78 us -> 4.31 us
    ppermute x1, waiting for transfers between devices: 0.72 us -> 0.3 us  [on_device(): b = lax.ppermute(b, 'row', odd_pairs(row_count))]
  transfers between devices with their start and end apart: 5 -> 5, of which waited for: 3 -> 3; matrix products, arithmetic and copies ran while one was open for 0% -> 0% of each run, Pallas kernels for 22% -> 23%
where the time goes in v2:
time: 21.6 us; the launch traced here: 21.5 us
  Pallas kernels  8.78 us (41%)
  starting transfers between devices  8.24 us (38%)
  waiting for transfers between devices  4.31 us (20%)
    ppermute x3, starting transfers between devices, on_device(): q.append(lax.ppermute(x, 'col', step[0]))  5.65 us
    ppermute x3, waiting for transfers between devices, on_device(): q.append(lax.ppermute(x, 'col', step[0]))  4 us
    pallas_call x1, Pallas kernels, on_device(): pl.pallas_call(functools.partial(local_kernel, count, low, where), out_sh...  2.94 us
    ppermute x1, starting transfers between devices, on_device(): b = lax.ppermute(b, 'row', odd_pairs(row_count))  2.54 us
    pallas_call x1, Pallas kernels, on_device(): pl.pallas_call(functools.partial(main_kernel, count, bands, where), out_s...  2.31 us
    pallas_call x1, Pallas kernels, on_device(): pl.pallas_call(functools.partial(stage_kernel, count, where, first), out_...  1.91 us
    pallas_call x1, Pallas kernels, on_device(): pl.pallas_call(functools.partial(pack_kernel, count, where), out_shape=[p...  1.23 us
  transfers between devices with their start and end apart: 5, of which 3 were waited for; matrix products, arithmetic and copies ran while one was open for 0% of the time, Pallas kernels for 23%

profile of v2, /device:TPU:0, one launch (start us, length us, event | category | flops | bytes accessed | tf_op | source)
XLA Modules:
  0.0 21.5 jit_solution(18357589909034482822)
XLA Ops:
  0.0 1.2 %pack.1 = (f32[104,128]{1,0:T(8,128)S(1)}, f32[104,128]{1,0:T(8,128)S(1)}, f32[80,128]{1,0:T(8,128)S(1)}) custom-call(f32[2,32,512]{2,1,0:T(8,128)} %ms_ref.1, f32[128,512]{1,0:T(8,128)} %last_ref.1, f32[128,512]{1,0:T(8,128)} %last_ref.1, bf16[64,256]{1,0:T(8,128)(2,1)} %constant.4.clone.table_ref), custom_call_target="tpu_custom_call" | custom-call | tf_op jit(solution)/shard_map/pack/pallas_call | solution.py:513
  1.2 4.1 %collective-permute-start.2 = (f32[80,128]{1,0:T(8,128)S(1)}, f32[80,128]{1,0:T(8,128)S(1)}, u32[]{:S(2)}, u32[]{:S(2)}) collective-permute-start(f32[80,128]{1,0:T(8,128)S(1)} %get-tuple-element.21), channel_id=1, source_target_pairs={{0,2},{1,3},{2,0},{3,1},{4,6},{5,7},{6,4},{7,5},{8,10},{9,11},{10,... | collective-permute-start | bytes 122888 | tf_op jit(solution)/shard_map/ppermute | solution.py:550
  5.3 1.6 %collective-permute-start = (f32[104,128]{1,0:T(8,128)S(1)}, f32[104,128]{1,0:T(8,128)S(1)}, u32[]{:S(2)}, u32[]{:S(2)}) collective-permute-start(f32[104,128]{1,0:T(8,128)S(1)} %get-tuple-element.19), channel_id=1, source_target_pairs={{0,1},{1,0},{2,3},{3,2},{4,5},{5,4},{6,7},{7,6},{8,9},{9,8},{10,11... | collective-permute-start | bytes 159752 | tf_op jit(solution)/shard_map/ppermute | solution.py:550
  6.9 0.0 copy-start
  6.9 0.0 collective-permute-start.1
  6.9 1.9 %stage.1 = (f32[80,128]{1,0:T(8,128)S(1)}, f32[96,128]{1,0:T(8,128)S(1)}, f32[96,128]{1,0:T(8,128)S(1)}, f32[128,512]{1,0:T(8,128)S(1)}, bf16[4832,256]{1,0:T(8,128)(2,1)S(1)}) custom-call(f32[2,32,512]{2,1,0:T(8,128)} %ms_ref.1, f32[128,512]{1,0:T(8,128)} %last_ref.1, bf16[4832,256]{1,0:T(8,128)(2,1)} %constant.5.clone.refs_2_), custom_call_target="tpu_custom_call" | custom-call | flops 1000000000 | bytes 1000000 | tf_op jit(solution)/shard_map/stage/pallas_call | solution.py:532
  8.8 0.0 collective-permute-done.2.refs_3_
  8.8 0.6 %collective-permute-done.refs_1_ = f32[104,128]{1,0:T(8,128)S(1)} collective-permute-done((f32[104,128]{1,0:T(8,128)S(1)}, f32[104,128]{1,0:T(8,128)S(1)}, u32[]{:S(2)}, u32[]{:S(2)}) %collective-permute-start) | collective-permute-done | bytes 53280 | tf_op jit(solution)/shard_map/ppermute | solution.py:550
  9.4 3.4 %collective-permute-done.1.refs_2_ = f32[104,128]{1,0:T(8,128)S(1)} collective-permute-done((f32[104,128]{1,0:T(8,128)S(1)}, f32[104,128]{1,0:T(8,128)S(1)}, u32[]{:S(2)}, u32[]{:S(2)}) %collective-permute-start.1) | collective-permute-done | bytes 53280 | tf_op jit(solution)/shard_map/ppermute | solution.py:550
  12.8 0.4 %rim.1 = (f32[280,128]{1,0:T(8,128)S(1)}, f32[234,128]{1,0:T(8,128)S(1)}, f32[128,128]{1,0:T(8,128)S(1)}) custom-call(f32[96,128]{1,0:T(8,128)S(1)} %get-tuple-element.23.top_ref, f32[96,128]{1,0:T(8,128)S(1)} %get-tuple-element.24.bot_ref, bf16[4832,256]{1,0:T(8,128)(2,1)S(1)} %get-tuple-element.25.table_ref.refs_7_.refs_3_, ...), custom_call_target="tpu_custom_call" | custom-call | tf_op jit(solution)/shard_map/rim/pallas_call | solution.py:552
  13.2 0.0 collective-permute-start.3
  13.3 0.0 copy-done
  13.3 0.1 copy.6.gains_ref
  13.4 2.5 %collective-permute-start.4 = (f32[234,128]{1,0:T(8,128)S(1)}, f32[234,128]{1,0:T(8,128)S(1)}, u32[]{:S(2)}, u32[]{:S(2)}) collective-permute-start(f32[234,128]{1,0:T(8,128)S(1)} %get-tuple-element.30), channel_id=1, source_target_pairs={{0,28},{4,8},{8,4},{12,16},{16,12},{20,24},{24,20},{28,0},{1,29},{... | collective-permute-start | bytes 359432 | tf_op jit(solution)/shard_map/ppermute | solution.py:561
  15.9 0.0 collective-permute-done.3.refs_6_
  15.9 2.9 %local.1 = (f32[8,128,512]{2,1,0:T(8,128)S(1)}, f32[24,512]{1,0:T(8,128)S(1)}) custom-call(f32[8,3]{1,0:T(8,128)S(1)} %copy.6.gains_ref, f32[80,128]{1,0:T(8,128)S(1)} %get-tuple-element.18.refs_0_, f32[104,128]{1,0:T(8,128)S(1)} %collective-permute-done.refs_1_, f32[104,128]{1,0:T(8,128)S(1)} %collective-permute-done.1.refs_2_, ...), custom_call_target="tpu_custom_call" | custom-call | flops 4000000000 | bytes 1000000 | tf_op jit(solution)/shard_map/local/pallas_call | solution.py:563
  18.8 0.3 %collective-permute-done.4.refs_2_ = f32[234,128]{1,0:T(8,128)S(1)} collective-permute-done((f32[234,128]{1,0:T(8,128)S(1)}, f32[234,128]{1,0:T(8,128)S(1)}, u32[]{:S(2)}, u32[]{:S(2)}) %collective-permute-start.4) | collective-permute-done | bytes 119840 | tf_op jit(solution)/shard_map/ppermute | solution.py:561
  19.1 2.3 %combine.1 = f32[8,128,512]{2,1,0:T(8,128)} custom-call(f32[8,128,512]{2,1,0:T(8,128)S(1)} %get-tuple-element.28.refs_0_, f32[24,512]{1,0:T(8,128)S(1)} %get-tuple-element.29.refs_1_, f32[234,128]{1,0:T(8,128)S(1)} %collective-permute-done.4.refs_2_, bf16[4832,256]{1,0:T(8,128)(2,1)S(1)} %get-tuple-element.25.table_ref.refs_7_.refs_3_), custom_call_target="tpu_custom_call" | custom-call | tf_op jit(solution)/shard_map/combine/pallas_call | solution.py:579
Async XLA Ops:
  1.2 7.6 %collective-permute-start.2 = (f32[80,128]{1,0:T(8,128)S(1)}, f32[80,128]{1,0:T(8,128)S(1)}, u32[]{:S(2)}, u32[]{:S(2)}) collective-permute-start(f32[80,128]{1,0:T(8,128)S(1)} %get-tuple-element.21), channel_id=1, source_target_pairs={{0,2},{1,3},{2,0},{3,1},{4,6},{5,7},{6,4},{7,5},{8,10},{9,11},{10,... | collective-permute-start | bytes 122888 | tf_op jit(solution)/shard_map/ppermute | solution.py:550
  5.3 4.1 %collective-permute-start = (f32[104,128]{1,0:T(8,128)S(1)}, f32[104,128]{1,0:T(8,128)S(1)}, u32[]{:S(2)}, u32[]{:S(2)}) collective-permute-start(f32[104,128]{1,0:T(8,128)S(1)} %get-tuple-element.19), channel_id=1, source_target_pairs={{0,1},{1,0},{2,3},{3,2},{4,5},{5,4},{6,7},{7,6},{8,9},{9,8},{10,11... | collective-permute-start | bytes 159752 | tf_op jit(solution)/shard_map/ppermute | solution.py:550
  6.9 6.4 %copy-start = (f32[8,3]{0,1:T(4,128)S(1)}, f32[8,3]{0,1:T(4,128)}, u32[]{:S(2)}) copy-start(f32[8,3]{0,1:T(4,128)} %param.7) | copy-start | bytes 292
  6.9 5.9 %collective-permute-start.1 = (f32[104,128]{1,0:T(8,128)S(1)}, f32[104,128]{1,0:T(8,128)S(1)}, u32[]{:S(2)}, u32[]{:S(2)}) collective-permute-start(f32[104,128]{1,0:T(8,128)S(1)} %get-tuple-element.20), channel_id=1, source_target_pairs={{0,3},{1,2},{2,1},{3,0},{4,7},{5,6},{6,5},{7,4},{8,11},{9,10},{10,... | collective-permute-start | bytes 159752 | tf_op jit(solution)/shard_map/ppermute | solution.py:550
  13.2 2.7 %collective-permute-start.3 = (f32[280,128]{1,0:T(8,128)S(1)}, f32[280,128]{1,0:T(8,128)S(1)}, u32[]{:S(2)}, u32[]{:S(2)}) collective-permute-start(f32[280,128]{1,0:T(8,128)S(1)} %get-tuple-element.27), channel_id=1, source_target_pairs={{0,4},{4,0},{8,12},{12,8},{16,20},{20,16},{24,28},{28,24},{1,5},{5... | collective-permute-start | bytes 430088 | tf_op jit(solution)/shard_map/ppermute | solution.py:560
  13.4 5.8 %collective-permute-start.4 = (f32[234,128]{1,0:T(8,128)S(1)}, f32[234,128]{1,0:T(8,128)S(1)}, u32[]{:S(2)}, u32[]{:S(2)}) collective-permute-start(f32[234,128]{1,0:T(8,128)S(1)} %get-tuple-element.30), channel_id=1, source_target_pairs={{0,28},{4,8},{8,4},{12,16},{16,12},{20,24},{24,20},{28,0},{1,29},{... | collective-permute-start | bytes 359432 | tf_op jit(solution)/shard_map/ppermute | solution.py:561

commit v3 on v2

--- a/solution.py
+++ b/solution.py
@@ -131,10 +131,11 @@
         assert not (ru_rims[0][:, : RIM - NEED] if side == 0 else ru_rims[1][:, NEED:]).any()
         used = ru_ends[side][:, RIM - NEED :] if side == 0 else ru_ends[side][:, :NEED]
         parts[f"end{side}"] = three(np.pad(used, ((0, 0), (0, RIM - NEED))))
-        gap = np.zeros((BAND_ROWS - REACH, COEFS))
-        for level in range(LEVELS):
-            m = edge[side][level]
-            parts[f"fix{level}{side}"] = three(np.concatenate([m, gap] if side == 0 else [gap, m]))
+        gap = np.zeros((BAND_ROWS - REACH, LEVELS * COEFS))
+        m = np.concatenate(edge[side], 1)
+        m = np.concatenate([m, gap] if side == 0 else [gap, m])
+        for name, x in zip(("fixhi", "fixlo"), split_const(m)):
+            parts[f"{name}{side}"] = np.concatenate([x] * 3, 1)
     for level in range(LEVELS):
         parts[f"own{level}"] = pair(own[level])
         parts[f"c1{level}hi"], parts[f"c1{level}lo"] = split_const(c1[level])
@@ -397,7 +398,7 @@
 
 def local_kernel(count, low, where, gains_ref, *refs):
     q, refs = refs[:count], refs[count:]
-    pan_ref, xh_ref, a_ref, table_ref, part_ref, gains_out, xe, tr, e3, mext, y_ref = refs
+    pan_ref, xh_ref, a_ref, table_ref, part_ref, fix_ref, xe, tr, e3, mext, y_ref = refs
     table = Table(table_ref, where)
     c, r = lax.axis_index("col"), lax.axis_index("row")
     below = lax.rem(r, 2) == 0
@@ -434,14 +435,21 @@
             hs = slice(h * half, (h + 1) * half)
             e3[level, :, hs] = (pan_ref[:, hs] if level == 0 else before[h]) - e
             before[h] = e
+    far_below = jnp.logical_not(below)
+    fix = table.side("fixhi", far_below).astype(F32) + table.side("fixlo", far_below).astype(F32)
+    lane = lanes((1, fix.shape[1]))
+    level_of = lax.rem(lane, LEVELS * COEFS) // COEFS
+    first_two = lanes(fix.shape) < 2 * LEVELS * COEFS
     for j in range(count):
         src = c if j == 0 else steps[j - 1][3](c)
         for i in range(bands):
             n = j * bands + i
             band = src * bands + i
             g1, g2, g3 = gains_ref[band, 0], gains_ref[band, 1], gains_ref[band, 2]
-            for k, g in enumerate((g1, g2, g3)):
-                gains_out[3 * n + k : 3 * n + k + 1, :] = jnp.full((1, cols), g, F32)
+            factor = jnp.where(level_of == 0, g2 - g1, jnp.where(level_of == 1, g3 - g2, -g3))
+            scaled = factor * fix
+            hi = scaled.astype(BF16).astype(F32)
+            fix_ref[n * BAND_ROWS : (n + 1) * BAND_ROWS, :] = jnp.where(first_two, hi, scaled - hi)
             part_ref[n] = (
                 dot(table.side("ru", below), three_high(y_ref[n * high : (n + 1) * high, :]))
                 + g1 * e3[0]
@@ -451,7 +459,7 @@
 
 
 def main_kernel(count, bands, where, *refs):
-    part_ref, gains_ref, b_ref, table_ref, out_ref, xe, de, mext, y_ref, obuf, sems = refs
+    part_ref, fix_ref, b_ref, table_ref, out_ref, xe, mext, y_ref, obuf, sems = refs
     table = Table(table_ref, where)
     c, r = lax.axis_index("col"), lax.axis_index("row")
     steps = column_steps(count)
@@ -467,8 +475,12 @@
         pltpu.make_async_copy(part_ref.at[n, done], out_ref.at[band[n], done], sems.at[0, n])
         for n in range(total)
     ]
-    for copy in copies:
-        copy.start()
+
+    @pl.loop(0, total)
+    def _(k):
+        at = sum(jnp.where(k == n, band[n], 0) for n in range(total))
+        pltpu.make_async_copy(part_ref.at[k, done], out_ref.at[at, done], sems.at[0, k]).start()
+
     height = blocks * COEFS
     band_rims(mext, b_ref, total, height + 8, RIM, 0, NEED)
     low_columns(mext, y_ref, table)
@@ -476,21 +488,25 @@
     tight = jnp.concatenate([pltpu.roll(packed, (-2 * RANK * g) % 128, 1) for g in range(3)], 0)
     corner = jnp.where(lanes(tight.shape) < COEFS, tight, pltpu.roll(tight, COEFS - RANK, 1))
     fill_rows(xe, slice(0, COEFS), cols, coef_piece(b_ref), corner)
-    before = [None, None]
-    for level in range(LEVELS):
-        for h, z in enumerate(columns(xe[...], cols, table, level)):
-            fix = dot(table.side(f"fix{level}", below), three_high(z))
-            de[level, :, h * half : (h + 1) * half] = -fix if level == 0 else before[h] - fix
-            before[h] = fix
+    x = xe[...]
+    levels = lambda name: tuple(
+        jnp.concatenate([table.two(name(level))[k] for level in range(LEVELS)], 1) for k in range(2)
+    )
+    z = rows3(split(jnp.concatenate([x[:, :half], x[:, half:cols]], 0)), levels(lambda level: f"c1{level}"))
+    wide = 2 * COEFS + REACH
+    parts = []
+    for h in range(2):
+        rim = split(x[:, cols + h * 128 : cols + h * 128 + wide])
+        parts.append(z[h * COEFS : (h + 1) * COEFS] + dot3(rim, levels(lambda level: f"c2{level}{h}")))
+    stacked = [
+        jnp.concatenate([p[:, level * half : (level + 1) * half] for p in parts], 1) for level in range(LEVELS)
+    ]
+    z = three_high(jnp.concatenate(stacked, 0))
+    fix = dot(fix_ref[...].astype(BF16), z)
     for n in range(total):
-        g = [gains_ref[3 * n + k : 3 * n + k + 1, :] for k in range(LEVELS)]
-        obuf[n] = (
-            part_ref[n, late, :]
-            + dot(table.side("end", below), three_high(y_ref[n * RIM : (n + 1) * RIM, :]))
-            + g[0] * de[0]
-            + g[1] * de[1]
-            + g[2] * de[2]
-        )
+        rim = three_high(y_ref[n * RIM : (n + 1) * RIM, :])
+        add = dot(table.side("end", below), rim) + fix[n * BAND_ROWS : (n + 1) * BAND_ROWS]
+        obuf[n] = part_ref[n, late, :] + add
         copy = pltpu.make_async_copy(obuf.at[n], out_ref.at[band[n], late], sems.at[1, n])
         copy.start()
         copies.append(copy)
@@ -562,7 +578,10 @@
     smem = pl.BlockSpec(memory_space=pltpu.SMEM)
     part, scaled = pl.pallas_call(
         functools.partial(local_kernel, count, low, where),
-        out_shape=[jax.ShapeDtypeStruct((total, rows, cols), F32), shape(LEVELS * total, cols)],
+        out_shape=[
+            jax.ShapeDtypeStruct((total, rows, cols), F32),
+            shape(total * BAND_ROWS, 3 * LEVELS * COEFS),
+        ],
         in_specs=[smem] + [whole] * (count + 4),
         out_specs=[whole] * 2,
         scratch_shapes=[
@@ -583,7 +602,6 @@
         out_specs=pl.BlockSpec(memory_space=pltpu.HBM),
         scratch_shapes=[
             VMEM((COEFS, cols + 256), F32),
-            VMEM((LEVELS, BAND_ROWS, cols), F32),
             VMEM((total * RIM, 256), F32),
             VMEM((total * RIM, cols), F32),
             VMEM((total, BAND_ROWS, cols), F32),

time: 21.6 us -> 21.2 us (0.981)
  Pallas kernels: 8.78 us -> 8.31 us
    pallas_call x1, Pallas kernels: 2.31 us -> 1.86 us  [on_device(): pl.pallas_call(functools.partial(main_kernel, count, bands, where), out_s...]
where the time goes in v3:
time: 21.2 us; the launch traced here: 21 us
  Pallas kernels  8.31 us (39%)
  starting transfers between devices  8.24 us (39%)
  waiting for transfers between devices  4.33 us (20%)
    ppermute x3, starting transfers between devices, on_device(): q.append(lax.ppermute(x, 'col', step[0]))  5.65 us
    ppermute x3, waiting for transfers between devices, on_device(): q.append(lax.ppermute(x, 'col', step[0]))  4.02 us
    pallas_call x1, Pallas kernels, on_device(): pl.pallas_call(functools.partial(local_kernel, count, low, where), out_sh...  2.94 us
    ppermute x1, starting transfers between devices, on_device(): b = lax.ppermute(b, 'row', odd_pairs(row_count))  2.54 us
    pallas_call x1, Pallas kernels, on_device(): pl.pallas_call(functools.partial(stage_kernel, count, where, first), out_...  1.89 us
    pallas_call x1, Pallas kernels, on_device(): pl.pallas_call(functools.partial(main_kernel, count, bands, where), out_s...  1.86 us
    pallas_call x1, Pallas kernels, on_device(): pl.pallas_call(functools.partial(pack_kernel, count, where), out_shape=[p...  1.23 us
  transfers between devices with their start and end apart: 5, of which 3 were waited for; matrix products, arithmetic and copies ran while one was open for 0% of the time, Pallas kernels for 23%

profile of v3, /device:TPU:0, one launch (start us, length us, event | category | flops | bytes accessed | tf_op | source)
XLA Modules:
  0.0 21.0 jit_solution(4993999458147034213)
XLA Ops:
  0.0 1.2 %pack.1 = (f32[104,128]{1,0:T(8,128)S(1)}, f32[104,128]{1,0:T(8,128)S(1)}, f32[80,128]{1,0:T(8,128)S(1)}) custom-call(f32[2,32,512]{2,1,0:T(8,128)} %ms_ref.1, f32[128,512]{1,0:T(8,128)} %last_ref.1, f32[128,512]{1,0:T(8,128)} %last_ref.1, bf16[64,256]{1,0:T(8,128)(2,1)} %constant.4.clone.table_ref), custom_call_target="tpu_custom_call" | custom-call | tf_op jit(solution)/shard_map/pack/pallas_call | solution.py:529
  1.2 4.1 %collective-permute-start.2 = (f32[80,128]{1,0:T(8,128)S(1)}, f32[80,128]{1,0:T(8,128)S(1)}, u32[]{:S(2)}, u32[]{:S(2)}) collective-permute-start(f32[80,128]{1,0:T(8,128)S(1)} %get-tuple-element.21), channel_id=1, source_target_pairs={{0,2},{1,3},{2,0},{3,1},{4,6},{5,7},{6,4},{7,5},{8,10},{9,11},{10,... | collective-permute-start | bytes 122888 | tf_op jit(solution)/shard_map/ppermute | solution.py:566
  5.3 1.6 %collective-permute-start = (f32[104,128]{1,0:T(8,128)S(1)}, f32[104,128]{1,0:T(8,128)S(1)}, u32[]{:S(2)}, u32[]{:S(2)}) collective-permute-start(f32[104,128]{1,0:T(8,128)S(1)} %get-tuple-element.19), channel_id=1, source_target_pairs={{0,1},{1,0},{2,3},{3,2},{4,5},{5,4},{6,7},{7,6},{8,9},{9,8},{10,11... | collective-permute-start | bytes 159752 | tf_op jit(solution)/shard_map/ppermute | solution.py:566
  6.9 0.0 copy-start
  6.9 0.0 collective-permute-start.1
  6.9 1.9 %stage.1 = (f32[80,128]{1,0:T(8,128)S(1)}, f32[96,128]{1,0:T(8,128)S(1)}, f32[96,128]{1,0:T(8,128)S(1)}, f32[128,512]{1,0:T(8,128)S(1)}, bf16[4704,256]{1,0:T(8,128)(2,1)S(1)}) custom-call(f32[2,32,512]{2,1,0:T(8,128)} %ms_ref.1, f32[128,512]{1,0:T(8,128)} %last_ref.1, bf16[4704,256]{1,0:T(8,128)(2,1)} %constant.5.clone.refs_2_), custom_call_target="tpu_custom_call" | custom-call | flops 1000000000 | bytes 1000000 | tf_op jit(solution)/shard_map/stage/pallas_call | solution.py:548
  8.8 0.0 collective-permute-done.2.refs_3_
  8.8 0.6 %collective-permute-done.refs_1_ = f32[104,128]{1,0:T(8,128)S(1)} collective-permute-done((f32[104,128]{1,0:T(8,128)S(1)}, f32[104,128]{1,0:T(8,128)S(1)}, u32[]{:S(2)}, u32[]{:S(2)}) %collective-permute-start) | collective-permute-done | bytes 53280 | tf_op jit(solution)/shard_map/ppermute | solution.py:566
  9.4 3.4 %collective-permute-done.1.refs_2_ = f32[104,128]{1,0:T(8,128)S(1)} collective-permute-done((f32[104,128]{1,0:T(8,128)S(1)}, f32[104,128]{1,0:T(8,128)S(1)}, u32[]{:S(2)}, u32[]{:S(2)}) %collective-permute-start.1) | collective-permute-done | bytes 53280 | tf_op jit(solution)/shard_map/ppermute | solution.py:566
  12.8 0.4 %rim.1 = (f32[280,128]{1,0:T(8,128)S(1)}, f32[234,128]{1,0:T(8,128)S(1)}, f32[128,128]{1,0:T(8,128)S(1)}) custom-call(f32[96,128]{1,0:T(8,128)S(1)} %get-tuple-element.23.top_ref, f32[96,128]{1,0:T(8,128)S(1)} %get-tuple-element.24.bot_ref, bf16[4704,256]{1,0:T(8,128)(2,1)S(1)} %get-tuple-element.25.table_ref.refs_7_.refs_3_, ...), custom_call_target="tpu_custom_call" | custom-call | tf_op jit(solution)/shard_map/rim/pallas_call | solution.py:568
  13.2 0.0 collective-permute-start.3
  13.3 0.0 copy-done
  13.3 0.1 copy.6.gains_ref
  13.4 2.5 %collective-permute-start.4 = (f32[234,128]{1,0:T(8,128)S(1)}, f32[234,128]{1,0:T(8,128)S(1)}, u32[]{:S(2)}, u32[]{:S(2)}) collective-permute-start(f32[234,128]{1,0:T(8,128)S(1)} %get-tuple-element.30), channel_id=1, source_target_pairs={{0,28},{4,8},{8,4},{12,16},{16,12},{20,24},{24,20},{28,0},{1,29},{... | collective-permute-start | bytes 359432 | tf_op jit(solution)/shard_map/ppermute | solution.py:577
  15.9 0.0 collective-permute-done.3.refs_6_
  15.9 2.9 %local.1 = (f32[8,128,512]{2,1,0:T(8,128)S(1)}, f32[448,216]{1,0:T(8,128)S(1)}) custom-call(f32[8,3]{1,0:T(8,128)S(1)} %copy.6.gains_ref, f32[80,128]{1,0:T(8,128)S(1)} %get-tuple-element.18.refs_0_, f32[104,128]{1,0:T(8,128)S(1)} %collective-permute-done.refs_1_, f32[104,128]{1,0:T(8,128)S(1)} %collective-permute-done.1.refs_2_, ...), custom_call_target="tpu_custom_call" | custom-call | flops 4000000000 | bytes 1000000 | tf_op jit(solution)/shard_map/local/pallas_call | solution.py:579
  18.8 0.3 %collective-permute-done.4.refs_2_ = f32[234,128]{1,0:T(8,128)S(1)} collective-permute-done((f32[234,128]{1,0:T(8,128)S(1)}, f32[234,128]{1,0:T(8,128)S(1)}, u32[]{:S(2)}, u32[]{:S(2)}) %collective-permute-start.4) | collective-permute-done | bytes 119840 | tf_op jit(solution)/shard_map/ppermute | solution.py:577
  19.1 1.9 %combine.1 = f32[8,128,512]{2,1,0:T(8,128)} custom-call(f32[8,128,512]{2,1,0:T(8,128)S(1)} %get-tuple-element.28.refs_0_, f32[448,216]{1,0:T(8,128)S(1)} %get-tuple-element.29.refs_1_, f32[234,128]{1,0:T(8,128)S(1)} %collective-permute-done.4.refs_2_, bf16[4704,256]{1,0:T(8,128)(2,1)S(1)} %get-tuple-element.25.table_ref.refs_7_.refs_3_), custom_call_target="tpu_custom_call" | custom-call | tf_op jit(solution)/shard_map/combine/pallas_call | solution.py:598
Async XLA Ops:
  1.2 7.6 %collective-permute-start.2 = (f32[80,128]{1,0:T(8,128)S(1)}, f32[80,128]{1,0:T(8,128)S(1)}, u32[]{:S(2)}, u32[]{:S(2)}) collective-permute-start(f32[80,128]{1,0:T(8,128)S(1)} %get-tuple-element.21), channel_id=1, source_target_pairs={{0,2},{1,3},{2,0},{3,1},{4,6},{5,7},{6,4},{7,5},{8,10},{9,11},{10,... | collective-permute-start | bytes 122888 | tf_op jit(solution)/shard_map/ppermute | solution.py:566
  5.3 4.1 %collective-permute-start = (f32[104,128]{1,0:T(8,128)S(1)}, f32[104,128]{1,0:T(8,128)S(1)}, u32[]{:S(2)}, u32[]{:S(2)}) collective-permute-start(f32[104,128]{1,0:T(8,128)S(1)} %get-tuple-element.19), channel_id=1, source_target_pairs={{0,1},{1,0},{2,3},{3,2},{4,5},{5,4},{6,7},{7,6},{8,9},{9,8},{10,11... | collective-permute-start | bytes 159752 | tf_op jit(solution)/shard_map/ppermute | solution.py:566
  6.9 6.4 %copy-start = (f32[8,3]{0,1:T(4,128)S(1)}, f32[8,3]{0,1:T(4,128)}, u32[]{:S(2)}) copy-start(f32[8,3]{0,1:T(4,128)} %param.7) | copy-start | bytes 292
  6.9 5.9 %collective-permute-start.1 = (f32[104,128]{1,0:T(8,128)S(1)}, f32[104,128]{1,0:T(8,128)S(1)}, u32[]{:S(2)}, u32[]{:S(2)}) collective-permute-start(f32[104,128]{1,0:T(8,128)S(1)} %get-tuple-element.20), channel_id=1, source_target_pairs={{0,3},{1,2},{2,1},{3,0},{4,7},{5,6},{6,5},{7,4},{8,11},{9,10},{10,... | collective-permute-start | bytes 159752 | tf_op jit(solution)/shard_map/ppermute | solution.py:566
  13.2 2.7 %collective-permute-start.3 = (f32[280,128]{1,0:T(8,128)S(1)}, f32[280,128]{1,0:T(8,128)S(1)}, u32[]{:S(2)}, u32[]{:S(2)}) collective-permute-start(f32[280,128]{1,0:T(8,128)S(1)} %get-tuple-element.27), channel_id=1, source_target_pairs={{0,4},{4,0},{8,12},{12,8},{16,20},{20,16},{24,28},{28,24},{1,5},{5... | collective-permute-start | bytes 430088 | tf_op jit(solution)/shard_map/ppermute | solution.py:576
  13.4 5.8 %collective-permute-start.4 = (f32[234,128]{1,0:T(8,128)S(1)}, f32[234,128]{1,0:T(8,128)S(1)}, u32[]{:S(2)}, u32[]{:S(2)}) collective-permute-start(f32[234,128]{1,0:T(8,128)S(1)} %get-tuple-element.30), channel_id=1, source_target_pairs={{0,28},{4,8},{8,4},{12,16},{16,12},{20,24},{24,20},{28,0},{1,29},{... | collective-permute-start | bytes 359432 | tf_op jit(solution)/shard_map/ppermute | solution.py:577
